TPU v7x, 32 devices: a whole 2x2x4 slice. The times are simulated.
32 devices in a mesh: grp: 2 (over y), frm: 4 (over z), row: 4 (over x, core).
Axes of the slice: x: 2, y: 2, z: 4, core: 2. Of those that a mesh axis runs over, the one named last changes fastest.
Arguments:
- queries: bfloat16 [16, 8, 128, 2240], P(('grp', 'frm'), 'row'), parts along dimension 0, may hold values from -6 to 6
- keys: bfloat16 [16, 8, 128, 2240], P(('grp', 'frm'), 'row'), parts along dimension 0, may hold values from -6 to 6
- values: bfloat16 [16, 8, 128, 2240], P(('grp', 'frm'), 'row'), parts along dimension 0, may hold values from -6 to 6
- flags: int32 [16], P(('grp', 'frm')), parts along dimension 0, may hold values 0 or 1
- blocks: int32 [16], P(('grp', 'frm')), parts along dimension 0, may hold values from 0 to 2, as said below
- out_weight: bfloat16 [2240, 2240], P('frm'), may hold values from -0.125 to 0.125
- norm_gain: float32 [2240], replicated, may hold values from 0.1 to 1.9
Outputs:
- projected: bfloat16 [16, 8, 128, 2240], P(('grp', 'frm'), 'row'), parts along dimension 0
There are 2 independent parts, one for each index of `grp`. A program takes and returns all parts, laid end to end along the dimension named above; an argument that names none is the same for every part. Nothing has to cross between parts.
Inputs may be any that keep to these rules, and one draw needn't show every extreme that they name: `flags`: 1 marks a clean frame, 0 a noisy one. `blocks`: within the 8 frames of one group, block numbers never fall and each block is 1 to 4 consecutive frames, some block exactly 4; every number from 0 to 2 occurs.
All inputs are finite; a program needn't handle non-finite values. No bound on the sum of `flags` on one device may be relied on, other than what follows from the above.
Results may differ from a plain program's by a relative error of at most 0.0049.
Values may be sent and summed in bfloat16 or wider, within the bound.
No kernel may reach another device: no remote copies, remote signals or barrier semaphores. Data moves between devices by JAX's collectives and lax.ppermute only.
A program may use at most 192 MiB of HBM per device.

v0:
```python
import jax
import jax.numpy as jnp
from jax import lax
from jax.sharding import PartitionSpec as P

HEADS = 20
HD = 112


norm_eps = 1e-06


def entering(part, axis, combine, identity):
    place = lax.axis_index(axis)
    gathered = jax.tree.map(lambda a: lax.all_gather(a, axis), part)
    state = jax.tree.map(lambda a, e: jnp.zeros_like(a) + jnp.asarray(e, a.dtype), part, identity)

    def one(step, state):
        return combine(
            state, jax.tree.map(lambda a: lax.dynamic_index_in_dim(a, step, 0, False), gathered)
        )

    return lax.fori_loop(0, place, one, state)


def combine(earlier, later):
    closed_a, opened_a, latest_a = earlier
    closed_b, opened_b, latest_b = later
    advance = (latest_a < latest_b).astype(jnp.float32)
    return (
        closed_a + closed_b + advance * opened_a,
        opened_b + (1.0 - advance) * opened_a,
        jnp.maximum(latest_a, latest_b),
    )


def empty_carry(length):
    return (
        jnp.zeros((length,), jnp.float32),
        jnp.zeros((length,), jnp.float32),
        jnp.full((1,), -1.0, jnp.float32),
    )


def frame_element(frame_states, flag_values, block_values, frame_idx):
    length = frame_states.shape[1]
    return (
        jnp.zeros((length,), jnp.float32),
        flag_values[frame_idx] * frame_states[frame_idx],
        block_values[frame_idx : frame_idx + 1],
    )


def fold_frames(frame_states, flag_values, block_values):
    running = empty_carry(frame_states.shape[1])
    for frame_idx in range(frame_states.shape[0]):
        running = combine(
            running, frame_element(frame_states, flag_values, block_values, frame_idx)
        )
    return running


def read_frames(prefix, frame_states, flag_values, block_values):
    running = prefix
    collected = []
    for frame_idx in range(frame_states.shape[0]):
        advance = (running[2] < block_values[frame_idx : frame_idx + 1]).astype(jnp.float32)
        select = jnp.maximum(advance, flag_values[frame_idx])
        collected.append(running[0] + select * running[1] + frame_states[frame_idx])
        running = combine(
            running, frame_element(frame_states, flag_values, block_values, frame_idx)
        )
    return jnp.stack(collected)


def local(queries, keys, values, flags, blocks, out_weight, norm_gain):
    frames, lat_rows, lat_cols, model_width = queries.shape
    tokens = lat_rows * lat_cols
    key_pos = jax.nn.relu(keys).reshape(frames, tokens, HEADS, HD)
    value_heads = values.reshape(frames, tokens, HEADS, HD)
    partial_value = jnp.einsum(
        "ftha,fthb->fhab", key_pos, value_heads, preferred_element_type=jnp.float32
    )
    partial_value = partial_value.reshape(frames, HEADS * HD * HD)
    flag_values = flags.astype(jnp.float32)
    block_values = blocks.astype(jnp.float32)
    summed = lax.psum(partial_value, "row")
    totals = fold_frames(summed, flag_values, block_values)
    prefix = entering(
        (totals[0], totals[1], totals[2]), "frm", combine, empty_carry(summed.shape[1])
    )
    read_states = read_frames(prefix, summed, flag_values, block_values)
    read_tensor = read_states.reshape(frames, HEADS, HD, HD)
    query_pos = jax.nn.relu(queries).reshape(frames, tokens, HEADS, HD).astype(jnp.float32)
    attended = jnp.einsum(
        "ftha,fhab->fthb", query_pos, read_tensor, precision=lax.Precision.HIGHEST
    )
    inv_rms = lax.rsqrt(jnp.mean(attended * attended, axis=-1, keepdims=True) + norm_eps)
    gain_table = norm_gain.reshape(HEADS, HD)
    normed = (
        (attended * inv_rms * gain_table).astype(jnp.bfloat16).reshape(frames * tokens, model_width)
    )
    projected = jnp.dot(
        normed,
        lax.all_gather(out_weight, "frm", axis=0, tiled=True),
        preferred_element_type=jnp.float32,
    )
    return projected.astype(jnp.bfloat16).reshape(frames, lat_rows, lat_cols, model_width)


def solution(mesh):
    in_specs = (
        P(("grp", "frm"), "row", None, None),
        P(("grp", "frm"), "row", None, None),
        P(("grp", "frm"), "row", None, None),
        P(("grp", "frm")),
        P(("grp", "frm")),
        P("frm", None),
        P(),
    )
    out_specs = P(("grp", "frm"), "row", None, None)
    return jax.shard_map(local, mesh=mesh, in_specs=in_specs, out_specs=out_specs, check_vma=False)
```

profile of v0, /device:TPU:0, one launch (start us, length us, event | category | flops | bytes accessed | tf_op | source)
XLA Modules:
  0.0 476.6 jit_solution(3732474962754750551)
XLA Ops:
  6.5 0.0 all-reduce.3.cloned.1.call-start
  6.5 1.8 broadcast_maximum_fusion.1
  8.3 10.3 %copy.16 = bf16[2,2,128,2240]{2,1,3,0:T(2,128)(2,1)} copy(bf16[2,2,128,2240]{2,3,1,0:T(8,128)(2,1)S(1)} %broadcast_maximum_fusion.1) | data formatting | bytes 4587520 | tf_op jit(solution)/shard_map/jit(relu)/max | solution.py:79
  18.7 5.2 %reshape.37 = bf16[2,256,20,112]{1,3,2,0:T(8,128)(2,1)S(1)} reshape(bf16[2,2,128,2240]{2,1,3,0:T(2,128)(2,1)} %copy.16) | data formatting | bytes 4587520 | tf_op jit(solution)/shard_map/reshape | solution.py:79
  23.9 12.6 %copy.17 = bf16[2,2,128,2240]{2,1,3,0:T(2,128)(2,1)} copy(bf16[2,2,128,2240]{2,3,1,0:T(8,128)(2,1)} %param.11) | data formatting | bytes 4587520 | tf_op args[2]
  36.5 6.2 %reshape.38 = bf16[2,256,20,112]{1,3,2,0:T(8,128)(2,1)} reshape(bf16[2,2,128,2240]{2,1,3,0:T(2,128)(2,1)} %copy.17) | data formatting | bytes 4587520 | tf_op jit(solution)/shard_map/reshape | solution.py:80
  42.7 3.8 fusion.10
  46.5 0.0 copy-start.3
  46.5 0.0 copy-start.5
  46.5 0.0 copy-start.4
  46.5 5.6 %reshape.39 = f32[2,250880]{1,0:T(2,128)} reshape(f32[2,20,112,112]{3,2,1,0:T(8,128)} %fusion.10) | data formatting | bytes 4014080 | tf_op jit(solution)/shard_map/reshape | solution.py:84
  52.0 0.0 all-reduce.3.cloned.1.call-update
  52.0 0.0 all-gather.11.cloned.1.call-start
  52.1 0.0 copy-done.3
  52.1 0.0 copy-done.5
  52.1 0.6 dynamic-slice
  52.7 1.3 maximum_dynamic-update-slice_fusion
  55.9 0.0 copy-done.4
  55.9 0.6 fusion.9
  56.6 48.6 %all-reduce.3.cloned.1.call-done = f32[2,250880]{1,0:T(2,128)} async-done(((f32[2,250880]{1,0:T(2,128)}), f32[2,250880]{1,0:T(2,128)}) %all-reduce.3.cloned.1.call-update) | async-done | bytes 2007056 | tf_op jit(solution)/shard_map/psum | solution.py:87
  105.1 8.0 %fusion.8 = (f32[1,250880]{1,0:T(1,128)S(1)}, f32[1,1,250880]{2,1,0:T(1,128)}, f32[1,1,250880]{2,1,0:T(1,128)}, f32[1,250880]{1,0:T(1,128)}) fusion(f32[2,250880]{1,0:T(2,128)} %all-reduce.3.cloned.1.call-done, f32[]{:T(128)} %bitcast.7, f32[]{:T(128)} %bitcast.6, f32[]{:T(128)} %bitcast.5, f32[]{:T(128)} %bitcast.12, f32[]{:T(128)} %bitcast.11), kind=kLoop, calls=%fused_computation.27 | loop fusion | flops 1505280 | bytes 6021140 | tf_op jit(solution)/shard_map/slice | solution.py:49
  113.1 0.0 copy-start.1
  113.1 0.0 all-gather.11.cloned.1.call-update
  113.1 0.0 all-gather.9.cloned.1.call-start
  113.1 0.7 all-gather.9.cloned.1.call-update
  113.8 0.0 all-gather.7.cloned.1.call-start
  113.9 0.5 all-gather.7.cloned.1.call-update
  114.4 11.9 %all-reduce = f32[4]{0:T(128)S(1)} all-reduce(f32[4]{0:T(128)S(1)} %get-tuple-element.81), channel_id=2, replica_groups=mesh['grp'=2,'frm'=4,'row'=4] {'frm'}, use_global_device_ids=true, to_apply=%add | all-reduce | flops 4 | bytes 32
  126.3 0.0 copy-done.1
  126.3 0.1 broadcast_maximum_fusion
  126.4 10.1 %copy.20 = bf16[2,2,128,2240]{2,1,3,0:T(2,128)(2,1)S(1)} copy(bf16[2,2,128,2240]{2,3,1,0:T(8,128)(2,1)S(1)} %broadcast_maximum_fusion) | data formatting | bytes 4587520 | tf_op jit(solution)/shard_map/jit(relu)/max | solution.py:94
  136.5 0.0 copy-start.2
  136.5 2.7 reshape.40
  139.3 0.0 copy-done.2
  139.3 0.1 mul.175
  139.3 51.7 %all-gather.11.cloned.1.call-done = f32[4,1,250880]{2,1,0:T(1,128)} async-done(((f32[1,1,250880]{2,1,0:T(1,128)}), f32[4,1,250880]{2,1,0:T(1,128)}) %all-gather.11.cloned.1.call-update) | async-done | bytes 4014096 | tf_op jit(solution)/shard_map/all_gather | solution.py:15
  191.1 5.5 %copy.28 = f32[4,1,250880]{2,0,1:T(4,128)} copy(f32[4,1,250880]{2,1,0:T(1,128)} %all-gather.11.cloned.1.call-done) | data formatting | bytes 8028160
  196.5 72.4 %all-gather.9.cloned.1.call-done = f32[4,1,250880]{2,1,0:T(1,128)} async-done(((f32[1,1,250880]{2,1,0:T(1,128)}), f32[4,1,250880]{2,1,0:T(1,128)}) %all-gather.9.cloned.1.call-update) | async-done | bytes 4014096 | tf_op jit(solution)/shard_map/all_gather | solution.py:15
  268.9 5.5 %copy.29 = f32[4,1,250880]{2,0,1:T(4,128)} copy(f32[4,1,250880]{2,1,0:T(1,128)} %all-gather.9.cloned.1.call-done) | data formatting | bytes 8028160
  274.4 0.1 broadcast.33
  274.5 0.1 broadcast.33.clone
  274.5 0.2 while.14
  277.9 3.6 add_add_fusion.1
  281.5 1.9 stack.9
  283.4 0.4 copy.18
  283.8 0.0 copy-start
  283.8 3.0 stack.10
  286.7 2.7 copy.19
  289.4 0.0 copy-done
  289.4 3.7 fusion
  293.2 0.7 fusion.2
  293.9 2.4 copy.21
  296.2 0.5 copy.25
  296.7 153.4 %all-gather.7.cloned.1.call-done = bf16[2240,2240]{1,0:T(8,128)(2,1)} async-done(((bf16[560,2240]{1,0:T(8,128)(2,1)}), bf16[2240,2240]{1,0:T(8,128)(2,1)}) %all-gather.7.cloned.1.call-update) | async-done | bytes 10035216 | tf_op jit(solution)/shard_map/all_gather | solution.py:105
  450.1 13.4 %convolution_convert_fusion = bf16[512,2240]{0,1:T(8,128)(2,1)} fusion(bf16[512,2240]{0,1:T(8,128)(2,1)S(1)} %bitcast.74, bf16[2240,2240]{1,0:T(8,128)(2,1)} %all-gather.7.cloned.1.call-done), kind=kOutput, calls=%fused_computation.10 | convolution fusion | flops 5139169280 | bytes 14622720 | tf_op jit(solution)/shard_map/dot_general | solution.py:103
  463.6 4.8 %reshape.42 = bf16[2,2,128,2240]{2,1,0,3:T(2,128)(2,1)S(1)} reshape(bf16[512,2240]{0,1:T(8,128)(2,1)} %convolution_convert_fusion) | data formatting | bytes 4587520 | tf_op jit(solution)/shard_map/reshape | solution.py:108
  468.4 1.7 copy.22
  (4 shorter events, 0.0 us)
Async XLA Ops:
  6.5 98.6 %all-reduce.3.cloned.1.call-start = ((), (), s32[]{:S(2)}) async-start(), calls=%async_computation | async-start | bytes 4014080 | tf_op jit(solution)/shard_map/psum | solution.py:87
  46.5 5.6 %copy-start.3 = (s32[2]{0:T(128)S(1)}, s32[2]{0:T(128)}, u32[]{:S(2)}) copy-start(s32[2]{0:T(128)} %param.13) | copy-start | bytes 28
  46.5 5.7 %copy-start.5 = (u32[32]{0:T(128)S(1)}, u32[32]{0:T(128)}, u32[]{:S(2)}) copy-start(u32[32]{0:T(128)} %constant.52) | copy-start | bytes 388
  46.5 9.4 %copy-start.4 = (s32[2]{0:T(128)S(1)}, s32[2]{0:T(128)}, u32[]{:S(2)}) copy-start(s32[2]{0:T(128)} %param.12) | copy-start | bytes 28
  52.0 139.0 %all-gather.11.cloned.1.call-start = ((), (), s32[]{:S(2)}) async-start(), calls=%async_computation.3 | async-start | bytes 5017600 | tf_op jit(solution)/shard_map/all_gather | solution.py:15
  113.1 13.2 %copy-start.1 = (bf16[2,2,128,2240]{2,3,1,0:T(8,128)(2,1)S(1)}, bf16[2,2,128,2240]{2,3,1,0:T(8,128)(2,1)}, u32[]{:S(2)}) copy-start(bf16[2,2,128,2240]{2,3,1,0:T(8,128)(2,1)} %param.9) | copy-start | bytes 6881284
  113.1 155.8 %all-gather.9.cloned.1.call-start = ((), (), s32[]{:S(2)}) async-start(), calls=%async_computation.2 | async-start | bytes 5017600 | tf_op jit(solution)/shard_map/all_gather | solution.py:15
  113.8 336.3 %all-gather.7.cloned.1.call-start = ((), (), s32[]{:S(2)}) async-start(), calls=%async_computation.1 | async-start | bytes 12902400 | tf_op jit(solution)/shard_map/all_gather | solution.py:105
  136.5 2.8 copy-start.2
  283.8 5.7 %copy-start = (bf16[2,256,20,112]{1,3,2,0:T(8,128)(2,1)S(1)}, bf16[2,256,20,112]{1,3,2,0:T(8,128)(2,1)}, u32[]{:S(2)}) copy-start(bf16[2,256,20,112]{1,3,2,0:T(8,128)(2,1)} %reshape.40) | copy-start | bytes 6881284
Sparse Core Ops, SparseCore 0:
  52.2 52.9 all-reduce.2
  113.2 77.8 all-gather.10
  192.6 76.2 all-gather.8
  270.3 179.7 all-gather.6
where the time goes:
time: 477 us
  waiting for transfers between devices  327 us (69%)
  local copies, waits for them, and re-layouts  82.4 us (17%)
  matrix products  21 us (4%)
  between operations  18.3 us (4%)
  other arithmetic  15.5 us (3%)
  blocking collectives  11.9 us (2%)
    all_gather x1, waiting for transfers between devices, local(): lax.all_gather(out_weight, 'frm', axis=0, tiled=True)  153 us
    all_gather x2, waiting for transfers between devices, entering(): gathered = jax.tree.map(lambda a: lax.all_gather(a, axis), part)  124 us
    psum x1, waiting for transfers between devices, local(): summed = lax.psum(partial_value, 'row')  48.6 us
    unnamed x18, local copies, waits for them, and re-layouts  24.6 us
    dot_general x1, matrix products, local(): jnp.dot(normed, lax.all_gather(out_weight, 'frm', axis=0, tiled=True), pr...  13.4 us
    unnamed x1, blocking collectives  11.9 us
    max x1, local copies, waits for them, and re-layouts, local(): key_pos = jax.nn.relu(keys).reshape(frames, tokens, HEADS, HD)  10.3 us
    max x1, local copies, waits for them, and re-layouts, local(): jax.nn.relu(queries).reshape(frames, tokens, HEADS, HD).astype(jnp.float32)  10.1 us
  transfers between devices with their start and end apart: 4, of which 4 were waited for; matrix products, arithmetic and copies ran while one was open for 10% of the time, Pallas kernels for 0%

commit v1 on v0

v1 whole, which is shorter than its diff:
```python
import functools

import jax
import jax.numpy as jnp
from jax import lax
from jax.experimental import pallas as pl
from jax.experimental.pallas import tpu as pltpu
from jax.sharding import PartitionSpec as P


HEADS = 20
HD = 112

norm_eps = 1e-06

STATES_VMEM = 64843328
SMALL_VMEM = 8 << 20
PROJECT_VMEM = 36 << 20
LANES = 128
LOADS = 4
BAND = 768


def ring(size, shift):
    return [(i, (i + shift) % size) for i in range(size)]


def side_by_side(ref, frame, rows):
    return jnp.concatenate([ref[frame, r, rows, :] for r in range(ref.shape[1])], axis=1)


def state_kernel(chips, heads_per, k_ref, v_ref, own_ref, sent_ref, *scratch):
    keys, values, exact, rounded, load_sem, sem = scratch
    row = lax.axis_index("row")
    chip, core = row // 2, lax.rem(row, 2)
    frames, _, width, _ = keys.shape
    per = width // LOADS
    loads = []
    for frame in range(frames):
        for part in range(LOADS):
            at = pl.ds(part * per, per)
            loads.append(
                [
                    pltpu.make_async_copy(
                        ref.at[frame, :, at], held.at[frame, :, at], load_sem.at[n, frame, part]
                    )
                    for n, (ref, held) in enumerate(((k_ref, keys), (v_ref, values)))
                ]
            )
    for pair in loads:
        for load in pair:
            load.start()
    for frame in range(frames):
        for head in range(HEADS):
            if head * HD % per == 0:
                for load in loads[frame * LOADS + head * HD // per]:
                    load.wait()
            at = slice(head * HD, (head + 1) * HD)
            state = lax.dot_general(
                side_by_side(values, frame, at),
                jnp.maximum(side_by_side(keys, frame, at), 0),
                (((1,), (1,)), ((), ())),
                preferred_element_type=jnp.float32,
            )
            exact[frame, head] = state
            rounded[frame, head] = state.astype(jnp.bfloat16)
        for head in range(HEADS, exact.shape[1]):
            exact[frame, head] = jnp.zeros((HD, HD), jnp.float32)
            rounded[frame, head] = jnp.zeros((HD, HD), jnp.bfloat16)
    copies = []
    for frame in range(frames):
        for step in range(chips):
            other = lax.rem(chip + step, chips) * 2
            mine = pl.ds((other + core) * heads_per, heads_per)
            theirs = pl.ds((other + 1 - core) * heads_per, heads_per)
            copies.append(
                pltpu.make_async_copy(
                    rounded.at[frame, theirs], sent_ref.at[step, frame], sem.at[1, frame, step]
                )
            )
            copies.append(
                pltpu.make_async_copy(
                    exact.at[frame, mine], own_ref.at[step, frame], sem.at[0, frame, step]
                )
            )
    for copy in copies:
        copy.start()
    for copy in copies:
        copy.wait()


def partial_states(keys, values, rows, heads_per):
    frames, _, _, _ = keys.shape
    chips = rows // 2
    far = pl.BlockSpec(memory_space=pltpu.MemorySpace.HBM)
    anywhere = pl.BlockSpec(memory_space=pl.ANY)
    piece = (chips, frames, heads_per, HD, HD)
    held = (frames, rows * heads_per, HD, HD)
    return pl.pallas_call(
        functools.partial(state_kernel, chips, heads_per),
        in_specs=[far, far],
        out_specs=[anywhere] * 2,
        scratch_shapes=[
            pltpu.VMEM(keys.shape, jnp.bfloat16),
            pltpu.VMEM(keys.shape, jnp.bfloat16),
            pltpu.VMEM(held, jnp.float32),
            pltpu.VMEM(held, jnp.bfloat16),
            pltpu.SemaphoreType.DMA((2, frames, LOADS)),
            pltpu.SemaphoreType.DMA((2, frames, chips)),
        ],
        out_shape=[
            jax.ShapeDtypeStruct(piece, jnp.float32),
            jax.ShapeDtypeStruct(piece, jnp.bfloat16),
        ],
        cost_estimate=pl.CostEstimate(
            flops=2 * keys.size * HD * 8, bytes_accessed=4 * keys.size, transcendentals=0
        ),
        compiler_params=pltpu.CompilerParams(vmem_limit_bytes=STATES_VMEM),
        name="states",
    )(keys, values)


def small(body, scalars, arrays, outs):
    scalar = pl.BlockSpec(memory_space=pltpu.SMEM)
    whole = pl.BlockSpec(memory_space=pltpu.VMEM)
    moved_bytes = sum(a.size * a.dtype.itemsize for a in arrays)
    return pl.pallas_call(
        body,
        in_specs=[scalar] * len(scalars) + [whole] * len(arrays),
        out_specs=[whole] * len(outs),
        out_shape=outs,
        cost_estimate=pl.CostEstimate(
            flops=moved_bytes, bytes_accessed=2 * moved_bytes, transcendentals=0
        ),
        compiler_params=pltpu.CompilerParams(vmem_limit_bytes=SMALL_VMEM),
    )(*scalars, *arrays)


def pair_kernel(own_ref, got_ref, mine_ref, *sent_refs):
    mine_ref[...] = own_ref[0] + got_ref[0].astype(jnp.float32)
    for step, sent_ref in enumerate(sent_refs, 1):
        total = own_ref[step] + got_ref[step].astype(jnp.float32)
        sent_ref[...] = total.astype(jnp.bfloat16)


def add_pair(own, got):
    shape = own.shape[1:]
    outs = [jax.ShapeDtypeStruct(shape, jnp.float32)]
    outs += [jax.ShapeDtypeStruct(shape, jnp.bfloat16)] * (own.shape[0] - 1)
    return small(pair_kernel, [], [own, got], outs)


def folded(flags, blocks, states, head):
    closed = jnp.zeros((HD, HD), jnp.float32)
    opened = flags[0].astype(jnp.float32) * states[0, head]
    for i in range(1, states.shape[0]):
        flag = flags[i].astype(jnp.float32)
        advance = (blocks[i - 1] < blocks[i]).astype(jnp.float32)
        closed, opened = (
            closed + advance * opened,
            flag * states[i, head] + (1.0 - advance) * opened,
        )
    return closed, opened


def joined(earlier, later, advance):
    return (
        earlier[0] + later[0] + advance * earlier[1],
        later[1] + (1.0 - advance) * earlier[1],
    )


def fold_kernel(flags, blocks, mine_ref, *rest):
    got_refs, (states_ref, carry_ref) = rest[:-2], rest[-2:]
    total = mine_ref[...]
    for got in got_refs:
        total = total + got[...].astype(jnp.float32)
    states_ref[...] = total
    for head in range(states_ref.shape[1]):
        closed, opened = folded(flags, blocks, states_ref, head)
        carry_ref[0, head] = closed.astype(jnp.bfloat16)
        carry_ref[1, head] = opened.astype(jnp.bfloat16)


def fold_states(flags, blocks, mine, got):
    outs = [
        jax.ShapeDtypeStruct(mine.shape, jnp.float32),
        jax.ShapeDtypeStruct((2,) + mine.shape[1:], jnp.bfloat16),
    ]
    return small(fold_kernel, [flags, blocks], [mine, *got], outs)


def join_kernel(has_prefix, sends, flags, blocks, near, far, states_ref, *rest):
    rest = list(rest)
    prefix_ref = rest.pop(0) if has_prefix else None
    got_ref = rest.pop(0)
    kept_ref = rest.pop(0) if has_prefix and sends else None
    out_ref = rest.pop(0)
    frames = states_ref.shape[0]
    before = near[frames - 1]
    for head in range(states_ref.shape[1]):
        prefix = (got_ref[0, head].astype(jnp.float32), got_ref[1, head].astype(jnp.float32))
        if has_prefix:
            advance = (far[frames - 1] < before).astype(jnp.float32)
            nearer = (
                prefix_ref[0, head].astype(jnp.float32),
                prefix_ref[1, head].astype(jnp.float32),
            )
            prefix = joined(prefix, nearer, advance)
        if sends:
            if has_prefix:
                kept_ref[0, head], kept_ref[1, head] = prefix
            advance = (before < blocks[frames - 1]).astype(jnp.float32)
            total = joined(prefix, folded(flags, blocks, states_ref, head), advance)
            out_ref[0, head] = total[0].astype(jnp.bfloat16)
            out_ref[1, head] = total[1].astype(jnp.bfloat16)
        else:
            closed, opened = prefix
            last = before
            for i in range(frames):
                flag = flags[i].astype(jnp.float32)
                advance = (last < blocks[i]).astype(jnp.float32)
                state = states_ref[i, head]
                read = closed + jnp.maximum(advance, flag) * opened + state
                out_ref[i, head] = read.astype(jnp.bfloat16)
                closed = closed + advance * opened
                opened = flag * state + (1.0 - advance) * opened
                last = blocks[i]


def join(flags, blocks, near, far, states, prefix, got, sends):
    arrays = [states] + ([] if prefix is None else [prefix]) + [got]
    outs = []
    if sends and prefix is not None:
        outs.append(jax.ShapeDtypeStruct(got.shape, jnp.float32))
    shape = got.shape if sends else states.shape
    outs.append(jax.ShapeDtypeStruct(shape, jnp.bfloat16))
    body = functools.partial(join_kernel, prefix is not None, sends)
    return small(body, [flags, blocks, near, far], arrays, outs)


def bands(width):
    edges = list(range(0, width, BAND)) + [width]
    return [slice(*pair) for pair in zip(edges, edges[1:])]


def project_kernel(chunks, pieces, table_of, q_ref, gain_ref, *rest):
    state_refs = rest[:chunks]
    weight_refs = rest[chunks : chunks + pieces]
    out_ref, states, weight, turned, normed, out, state_sem, out_sem = rest[chunks + pieces :]
    frames, lat_rows, width, lat_cols = q_ref.shape
    tokens = lat_rows * lat_cols
    heads_per = states.shape[2]
    held, offsets = table_of(*(lax.axis_index(name) for name in ("grp", "frm", "row")))
    state_copies = [
        pltpu.make_async_copy(state_refs[n], states.at[held[n]], state_sem.at[n])
        for n in range(chunks)
    ]
    for copy in state_copies:
        copy.start()
    for ref, (row, column) in zip(weight_refs, offsets):
        at = pl.ds(pl.multiple_of(row, 16), ref.shape[0])
        weight[at, pl.ds(pl.multiple_of(column, LANES), ref.shape[1])] = ref[...]
    for copy in state_copies:
        copy.wait()
    gains = gain_ref[...].T
    for head in range(HEADS):
        chunk, slot = divmod(head, heads_per)
        at = slice(head * HD, (head + 1) * HD)
        gain = gains[:, head : head + 1]
        for frame in range(frames):
            attended = jnp.dot(
                states[chunk, frame, slot],
                jnp.maximum(side_by_side(q_ref, frame, at), 0),
                preferred_element_type=jnp.float32,
            )
            mean = jnp.mean(attended * attended, axis=0, keepdims=True)
            scaled = attended * lax.rsqrt(mean + norm_eps) * gain
            turned[at, frame * tokens : (frame + 1) * tokens] = scaled.astype(jnp.bfloat16)
    for start in range(0, width, 256):
        at = slice(start, min(start + 256, width))
        normed[:, at] = turned[at, :].T
    stores = []
    for b, band in enumerate(bands(width)):
        for start in range(band.start, band.stop, 256):
            at = slice(start, min(start + 256, band.stop))
            result = jnp.dot(normed[...], weight[:, at], preferred_element_type=jnp.float32)
            result = result.astype(jnp.bfloat16).T
            for frame in range(frames):
                for r in range(lat_rows):
                    first = frame * tokens + r * lat_cols
                    out[frame, r, at, :] = result[:, first : first + lat_cols]
        stores.append(
            pltpu.make_async_copy(out.at[:, :, band], out_ref.at[:, :, band], out_sem.at[b])
        )
        stores[-1].start()
    for store in stores:
        store.wait()


def project(queries, gain, states, weights, table_of):
    chunks, pieces = len(states), len(weights)
    frames, lat_rows, width, lat_cols = queries.shape
    tokens = frames * lat_rows * lat_cols
    anywhere = pl.BlockSpec(memory_space=pl.ANY)
    far = pl.BlockSpec(memory_space=pltpu.MemorySpace.HBM)
    whole = pl.BlockSpec(memory_space=pltpu.VMEM)
    count = len(bands(width))
    return pl.pallas_call(
        functools.partial(project_kernel, chunks, pieces, table_of),
        in_specs=[whole, whole] + [anywhere] * chunks + [whole] * pieces,
        out_specs=far,
        scratch_shapes=[
            pltpu.VMEM((chunks,) + states[0].shape, jnp.bfloat16),
            pltpu.VMEM((width, -(-width // LANES) * LANES), jnp.bfloat16),
            pltpu.VMEM((width, tokens), jnp.bfloat16),
            pltpu.VMEM((tokens, width), jnp.bfloat16),
            pltpu.VMEM(queries.shape, jnp.bfloat16),
            pltpu.SemaphoreType.DMA((chunks,)),
            pltpu.SemaphoreType.DMA((count,)),
        ],
        out_shape=jax.ShapeDtypeStruct(queries.shape, jnp.bfloat16),
        cost_estimate=pl.CostEstimate(
            flops=2 * queries.size * (width + 4 * HD),
            bytes_accessed=2 * (2 * queries.size + width * width),
            transcendentals=0,
        ),
        compiler_params=pltpu.CompilerParams(vmem_limit_bytes=PROJECT_VMEM),
        name="project",
    )(queries, gain, *states, *weights)


def gather_weight(weight, sizes, places):
    groups, frms, rows = sizes
    grp, _, row = places
    own_rows, width = weight.shape
    chips = rows // 2
    members = groups * chips
    half = -(-width // (2 * LANES)) * LANES
    piece_rows = -(-own_rows // (16 * members)) * 16
    if own_rows % 16 or piece_rows > own_rows or half >= width:
        whole = lax.all_gather(weight, "frm", axis=0, tiled=True)
        return [whole], lambda grp, frm, row: [(frm * 0, frm * 0)]

    def first_row(number):
        over = members * piece_rows - own_rows
        assert over < piece_rows
        return number * piece_rows - (number + 1) // members * over

    start = first_row(grp * chips + row // 2)
    lines = lax.dynamic_slice_in_dim(weight, start, piece_rows, 0)
    right = jnp.pad(lines[:, half:], ((0, 0), (0, 2 * half - width)))
    piece = jnp.where(row % 2 == 0, lines[:, :half], right)
    arrays, plan, reached = [weight], [], {}
    cores = [(i, i ^ 1) for i in range(rows)]
    order = sorted(range(1, frms), key=lambda s: min(s, frms - s))
    for turn, shift in enumerate(order):
        hop = 1 if 2 * shift <= frms else -1
        behind = reached.get(shift - hop, piece)
        first = lax.ppermute(behind, "frm", ring(frms, hop))
        reached[shift] = first
        held = {(0, 0): first}
        for axis in ("row", "grp") if turn else ("grp", "row"):
            for (dg, dx), block in list(held.items()):
                if axis == "grp":
                    for s in range(1, groups):
                        held[(dg + s, dx)] = lax.ppermute(block, "grp", ring(groups, s))
                else:
                    for s in range(1, chips):
                        held[(dg, dx + s)] = lax.ppermute(block, "row", ring(rows, 2 * s))
        for (dg, dx), block in held.items():
            arrays.append(block)
            arrays.append(lax.ppermute(block, "row", cores))
            plan.append((shift, dg, dx))

    def offsets(grp, frm, row):
        chip, core = row // 2, lax.rem(row, 2)
        starts = [(frm * own_rows, frm * 0)]
        for shift, dg, dx in plan:
            base = lax.rem(frm + frms - shift, frms) * own_rows
            g, x = lax.rem(grp + groups - dg, groups), lax.rem(chip + chips - dx, chips)
            at = base + first_row(g * chips + x)
            starts += [(at, core * half), (at, (1 - core) * half)]
        return starts

    return arrays, offsets


def local(sizes, *args):
    return attention(sizes, *args)


def attention(sizes, queries, keys, values, flags, blocks, out_weight, norm_gain):
    _, frms, rows = sizes
    chips = rows // 2
    places = tuple(lax.axis_index(name) for name in ("grp", "frm", "row"))
    heads_per = -(-HEADS // rows)
    queries, keys, values = (a.transpose(0, 1, 3, 2) for a in (queries, keys, values))
    cores = [(i, i ^ 1) for i in range(rows)]

    def chip_pairs(step):
        return [(i, (i + 2 * step) % rows) for i in range(rows)]

    def ahead(reach):
        return [(i, i + reach) for i in range(frms - reach)]

    weights, offsets_of = gather_weight(out_weight, sizes, places)

    own, sent = partial_states(keys, values, rows, heads_per)
    mine, *sends = add_pair(own, lax.ppermute(sent, "row", cores))
    got = [lax.ppermute(a, "row", chip_pairs(s)) for s, a in enumerate(sends, 1)]
    near = lax.ppermute(blocks, "frm", ahead(1))
    states, carry = fold_states(flags, blocks, mine, got)

    prefix, reach, far = None, 1, near
    while True:
        got = lax.ppermute(carry, "frm", ahead(reach))
        last = 2 * reach >= frms
        out = join(flags, blocks, near, far, states, prefix, got, not last)
        if last:
            read = out[0]
            break
        carry = out[-1]
        prefix = got if prefix is None else out[0]
        reach *= 2
        far = lax.ppermute(blocks, "frm", ahead(reach))

    shared = [read]
    for step in range(1, chips):
        shared.append(lax.ppermute(read, "row", chip_pairs(step)))
    reads = []
    for array in shared:
        reads += [array, lax.ppermute(array, "row", cores)]

    def table_of(grp, frm, row):
        chip, core = row // 2, lax.rem(row, 2)
        held = []
        for step in range(chips):
            other = lax.rem(chip + chips - step, chips) * 2
            held += [other + core, other + 1 - core]
        return held, offsets_of(grp, frm, row)

    gains = norm_gain.reshape(HEADS, HD)
    projected = project(queries, gains, reads, weights, table_of)
    return projected.transpose(0, 1, 3, 2)


def solution(mesh):
    sizes = tuple(mesh.shape[name] for name in ("grp", "frm", "row"))
    in_specs = (
        P(("grp", "frm"), "row", None, None),
        P(("grp", "frm"), "row", None, None),
        P(("grp", "frm"), "row", None, None),
        P(("grp", "frm")),
        P(("grp", "frm")),
        P("frm", None),
        P(),
    )
    out_specs = P(("grp", "frm"), "row", None, None)
    return jax.shard_map(
        functools.partial(local, sizes),
        mesh=mesh,
        in_specs=in_specs,
        out_specs=out_specs,
        check_vma=False,
    )
```

time: 477 us -> 118 us (0.25)
  the two profiles are of different devices: /device:TPU:0 before, /device:TPU:25 now
where the time goes in v1:
time: 118 us; the launch traced here: 117 us
  starting transfers between devices  39.1 us (33%)
  waiting for transfers between devices  35 us (30%)
  local copies, waits for them, and re-layouts  24 us (20%)
  Pallas kernels  17.8 us (15%)
    unnamed x76, local copies, waits for them, and re-layouts  23 us
    ppermute x12, starting transfers between devices, gather_weight(): arrays.append(lax.ppermute(block, 'row', cores))  16.3 us
    ppermute x2, waiting for transfers between devices, attention(): got = lax.ppermute(carry, 'frm', ahead(reach))  11.4 us
    pallas_call x1, Pallas kernels, project(): pl.pallas_call(functools.partial(project_kernel, chunks, pieces, table_of...  11.1 us
    ppermute x4, waiting for transfers between devices, gather_weight(): held[dg, dx + s] = lax.ppermute(block, 'row', ring(rows, 2 * s))  5.2 us
    ppermute x1, waiting for transfers between devices, attention(): far = lax.ppermute(blocks, 'frm', ahead(reach))  4.77 us
    ppermute x5, starting transfers between devices, gather_weight(): held[dg + s, dx] = lax.ppermute(block, 'grp', ring(groups, s))  4.63 us
    ppermute x3, starting transfers between devices, gather_weight(): first = lax.ppermute(behind, 'frm', ring(frms, hop))  4.56 us
  transfers between devices with their start and end apart: 33, of which 10 were waited for; matrix products, arithmetic and copies ran while one was open for 0% of the time, Pallas kernels for 6%

profile of v1, /device:TPU:25, one launch (start us, length us, event | category | flops | bytes accessed | tf_op | source)
XLA Modules:
  0.0 117.3 jit_solution(16831179157767892064)
XLA Ops:
  0.0 1.0 dynamic-slice.1
  1.0 1.1 dynamic-slice_select_fusion
  2.3 4.5 %states.1 = (f32[2,2,5,112,112]{4,3,2,1,0:T(8,128)}, bf16[2,2,5,112,112]{4,3,2,1,0:T(8,128)(2,1)}) custom-call(bf16[2,2,2240,128]{3,2,1,0:T(8,128)(2,1)} %bitcast.5, bf16[2,2,2240,128]{3,2,1,0:T(8,128)(2,1)} %bitcast.6), custom_call_target="tpu_custom_call" | custom-call | flops 2055208960 | bytes 4587520 | tf_op jit(solution)/shard_map/states/pallas_call | solution.py:99
  6.8 1.0 collective-permute-start.2
  7.8 3.1 %collective-permute-start.9 = (bf16[144,1152]{1,0:T(8,128)(2,1)S(1)}, bf16[144,1152]{1,0:T(8,128)(2,1)S(1)}, u32[]{:S(2)}, u32[]{:S(2)}) collective-permute-start(bf16[144,1152]{1,0:T(8,128)(2,1)S(1)} %dynamic-slice_select_fusion), channel_id=1, source_target_pairs={{0,4},{4,8},{8,12},{12,0},{1,5},{5,9},{9,13},{13,1},{2,6},{6,10},{... | collective-permute-start | bytes 995336 | tf_op jit(solution)/shard_map/ppermute | solution.py:360
  10.9 1.7 %collective-permute-done.17.rest_13_ = bf16[144,1152]{1,0:T(8,128)(2,1)S(1)} collective-permute-done((bf16[144,1152]{1,0:T(8,128)(2,1)S(1)}, bf16[144,1152]{1,0:T(8,128)(2,1)S(1)}, u32[]{:S(2)}, u32[]{:S(2)}) %collective-permute-start.17) | collective-permute-done | bytes 331808 | tf_op jit(solution)/shard_map/ppermute | solution.py:360
  12.7 1.2 %collective-permute-start.21 = (bf16[144,1152]{1,0:T(8,128)(2,1)S(1)}, bf16[144,1152]{1,0:T(8,128)(2,1)S(1)}, u32[]{:S(2)}, u32[]{:S(2)}) collective-permute-start(bf16[144,1152]{1,0:T(8,128)(2,1)S(1)} %collective-permute-done.17.rest_13_), channel_id=1, source_target_pairs={{0,16},{16,0},{1,17},{17,1},{2,18},{18,2},{3,19},{19,3},{4,20},{20... | collective-permute-start | bytes 995336 | tf_op jit(solution)/shard_map/ppermute | solution.py:367
  13.9 1.2 %collective-permute-start.19 = (bf16[144,1152]{1,0:T(8,128)(2,1)S(1)}, bf16[144,1152]{1,0:T(8,128)(2,1)S(1)}, u32[]{:S(2)}, u32[]{:S(2)}) collective-permute-start(bf16[144,1152]{1,0:T(8,128)(2,1)S(1)} %collective-permute-done.17.rest_13_), channel_id=1, source_target_pairs={{0,2},{1,3},{2,0},{3,1},{4,6},{5,7},{6,4},{7,5},{8,10},{9,11},{10,... | collective-permute-start | bytes 995336 | tf_op jit(solution)/shard_map/ppermute | solution.py:370
  15.1 3.2 %collective-permute-start.18 = (bf16[144,1152]{1,0:T(8,128)(2,1)S(1)}, bf16[144,1152]{1,0:T(8,128)(2,1)S(1)}, u32[]{:S(2)}, u32[]{:S(2)}) collective-permute-start(bf16[144,1152]{1,0:T(8,128)(2,1)S(1)} %collective-permute-done.17.rest_13_), channel_id=1, source_target_pairs={{0,1},{1,0},{2,3},{3,2},{4,5},{5,4},{6,7},{7,6},{8,9},{9,8},{10,11... | collective-permute-start | bytes 995336 | tf_op jit(solution)/shard_map/ppermute | solution.py:373
  18.3 2.4 %collective-permute-done.9.rest_5_ = bf16[144,1152]{1,0:T(8,128)(2,1)S(1)} collective-permute-done((bf16[144,1152]{1,0:T(8,128)(2,1)S(1)}, bf16[144,1152]{1,0:T(8,128)(2,1)S(1)}, u32[]{:S(2)}, u32[]{:S(2)}) %collective-permute-start.9) | collective-permute-done | bytes 331808 | tf_op jit(solution)/shard_map/ppermute | solution.py:360
  20.8 1.2 %collective-permute-start.25 = (bf16[144,1152]{1,0:T(8,128)(2,1)S(1)}, bf16[144,1152]{1,0:T(8,128)(2,1)S(1)}, u32[]{:S(2)}, u32[]{:S(2)}) collective-permute-start(bf16[144,1152]{1,0:T(8,128)(2,1)S(1)} %collective-permute-done.9.rest_5_), channel_id=1, source_target_pairs={{0,4},{4,8},{8,12},{12,0},{1,5},{5,9},{9,13},{13,1},{2,6},{6,10},{... | collective-permute-start | bytes 995336 | tf_op jit(solution)/shard_map/ppermute | solution.py:360
  22.0 1.3 %collective-permute-start.1 = (s32[2]{0:T(128)S(1)}, s32[2]{0:T(128)S(1)}, u32[]{:S(2)}, u32[]{:S(2)}) collective-permute-start(s32[2]{0:T(128)S(1)} %copy-done.3), channel_id=1, source_target_pairs={{0,8},{4,12},{1,9},{5,13},{2,10},{6,14},{3,11},{7,15},{16,24},{20,... | collective-permute-start | bytes 32 | tf_op jit(solution)/shard_map/ppermute | solution.py:426
  23.3 1.2 %copy-done = f32[2,2,5,112,112]{4,3,2,1,0:T(8,128)S(1)} copy-done((f32[2,2,5,112,112]{4,3,2,1,0:T(8,128)S(1)}, f32[2,2,5,112,112]{4,3,2,1,0:T(8,128)}, u32[]{:S(2)}) %copy-start) | copy-done | bytes 1003544
  24.7 4.8 %collective-permute-done.1.far = s32[2]{0:T(128)S(1)} collective-permute-done((s32[2]{0:T(128)S(1)}, s32[2]{0:T(128)S(1)}, u32[]{:S(2)}, u32[]{:S(2)}) %collective-permute-start.1) | collective-permute-done | bytes 40 | tf_op jit(solution)/shard_map/ppermute | solution.py:426
  29.4 1.3 %collective-permute-start = (s32[2]{0:T(128)S(1)}, s32[2]{0:T(128)S(1)}, u32[]{:S(2)}, u32[]{:S(2)}) collective-permute-start(s32[2]{0:T(128)S(1)} %copy-done.3), channel_id=1, source_target_pairs={{0,4},{4,8},{8,12},{1,5},{5,9},{9,13},{2,6},{6,10},{10,14},{3,7},{... | collective-permute-start | bytes 32 | tf_op jit(solution)/shard_map/ppermute | solution.py:412
  30.7 3.0 %collective-permute-done.near.far = s32[2]{0:T(128)S(1)} collective-permute-done((s32[2]{0:T(128)S(1)}, s32[2]{0:T(128)S(1)}, u32[]{:S(2)}, u32[]{:S(2)}) %collective-permute-start) | collective-permute-done | bytes 40 | tf_op jit(solution)/shard_map/ppermute | solution.py:412
  33.8 1.2 %collective-permute-start.3 = (bf16[2,5,112,112]{3,2,1,0:T(8,128)(2,1)S(1)}, bf16[2,5,112,112]{3,2,1,0:T(8,128)(2,1)S(1)}, u32[]{:S(2)}, u32[]{:S(2)}) collective-permute-start(bf16[2,5,112,112]{3,2,1,0:T(8,128)(2,1)S(1)} %get-tuple-element.14), channel_id=1, source_target_pairs={{0,2},{1,3},{2,0},{3,1},{4,6},{5,7},{6,4},{7,5},{8,10},{9,11},{10,... | collective-permute-start | bytes 752648 | tf_op jit(solution)/shard_map/ppermute | solution.py:411
  35.2 1.2 %collective-permute-start.11 = (bf16[144,1152]{1,0:T(8,128)(2,1)S(1)}, bf16[144,1152]{1,0:T(8,128)(2,1)S(1)}, u32[]{:S(2)}, u32[]{:S(2)}) collective-permute-start(bf16[144,1152]{1,0:T(8,128)(2,1)S(1)} %collective-permute-done.9.rest_5_), channel_id=1, source_target_pairs={{0,16},{16,0},{1,17},{17,1},{2,18},{18,2},{3,19},{19,3},{4,20},{20... | collective-permute-start | bytes 995336 | tf_op jit(solution)/shard_map/ppermute | solution.py:367
  36.5 0.7 copy-done.9
  37.2 3.6 %collective-permute-start.10 = (bf16[144,1152]{1,0:T(8,128)(2,1)S(1)}, bf16[144,1152]{1,0:T(8,128)(2,1)S(1)}, u32[]{:S(2)}, u32[]{:S(2)}) collective-permute-start(bf16[144,1152]{1,0:T(8,128)(2,1)S(1)} %collective-permute-done.9.rest_5_), channel_id=1, source_target_pairs={{0,1},{1,0},{2,3},{3,2},{4,5},{5,4},{6,7},{7,6},{8,9},{9,8},{10,11... | collective-permute-start | bytes 995336 | tf_op jit(solution)/shard_map/ppermute | solution.py:373
  41.1 0.7 shard_map.74
  41.8 4.7 %collective-permute-done.13.rest_9_ = bf16[144,1152]{1,0:T(8,128)(2,1)S(1)} collective-permute-done((bf16[144,1152]{1,0:T(8,128)(2,1)S(1)}, bf16[144,1152]{1,0:T(8,128)(2,1)S(1)}, u32[]{:S(2)}, u32[]{:S(2)}) %collective-permute-start.13) | collective-permute-done | bytes 331808 | tf_op jit(solution)/shard_map/ppermute | solution.py:370
  46.5 1.3 %collective-permute-start.4 = (bf16[2,5,112,112]{3,2,1,0:T(8,128)(2,1)S(1)}, bf16[2,5,112,112]{3,2,1,0:T(8,128)(2,1)S(1)}, u32[]{:S(2)}, u32[]{:S(2)}) collective-permute-start(bf16[2,5,112,112]{3,2,1,0:T(8,128)(2,1)S(1)} %get-tuple-element.16), channel_id=1, source_target_pairs={{0,4},{4,8},{8,12},{1,5},{5,9},{9,13},{2,6},{6,10},{10,14},{3,7},{... | collective-permute-start | bytes 752648 | tf_op jit(solution)/shard_map/ppermute | solution.py:417
  47.8 3.7 %collective-permute-start.20 = (bf16[144,1152]{1,0:T(8,128)(2,1)S(1)}, bf16[144,1152]{1,0:T(8,128)(2,1)S(1)}, u32[]{:S(2)}, u32[]{:S(2)}) collective-permute-start(bf16[144,1152]{1,0:T(8,128)(2,1)S(1)} %collective-permute-done.19.rest_15_), channel_id=1, source_target_pairs={{0,1},{1,0},{2,3},{3,2},{4,5},{5,4},{6,7},{7,6},{8,9},{9,8},{10,11... | collective-permute-start | bytes 995336 | tf_op jit(solution)/shard_map/ppermute | solution.py:373
  51.5 0.7 copy-done.17
  52.2 1.2 %collective-permute-start.29 = (bf16[144,1152]{1,0:T(8,128)(2,1)S(1)}, bf16[144,1152]{1,0:T(8,128)(2,1)S(1)}, u32[]{:S(2)}, u32[]{:S(2)}) collective-permute-start(bf16[144,1152]{1,0:T(8,128)(2,1)S(1)} %collective-permute-done.25.rest_21_), channel_id=1, source_target_pairs={{0,16},{16,0},{1,17},{17,1},{2,18},{18,2},{3,19},{19,3},{4,20},{20... | collective-permute-start | bytes 995336 | tf_op jit(solution)/shard_map/ppermute | solution.py:367
  53.5 0.7 copy-done.19
  54.2 1.2 %collective-permute-start.27 = (bf16[144,1152]{1,0:T(8,128)(2,1)S(1)}, bf16[144,1152]{1,0:T(8,128)(2,1)}, u32[]{:S(2)}, u32[]{:S(2)}) collective-permute-start(bf16[144,1152]{1,0:T(8,128)(2,1)S(1)} %collective-permute-done.25.rest_21_), channel_id=1, source_target_pairs={{0,2},{1,3},{2,0},{3,1},{4,6},{5,7},{6,4},{7,5},{8,10},{9,11},{10,... | collective-permute-start | bytes 995336 | tf_op jit(solution)/shard_map/ppermute | solution.py:370
  55.4 0.6 collective-permute-start.26
  56.0 2.6 %collective-permute-start.14 = (bf16[144,1152]{1,0:T(8,128)(2,1)S(1)}, bf16[144,1152]{1,0:T(8,128)(2,1)S(1)}, u32[]{:S(2)}, u32[]{:S(2)}) collective-permute-start(bf16[144,1152]{1,0:T(8,128)(2,1)S(1)} %collective-permute-done.13.rest_9_), channel_id=1, source_target_pairs={{0,1},{1,0},{2,3},{3,2},{4,5},{5,4},{6,7},{7,6},{8,9},{9,8},{10,11... | collective-permute-start | bytes 995336 | tf_op jit(solution)/shard_map/ppermute | solution.py:373
  58.6 0.7 shard_map.75
  59.4 1.3 %collective-permute-start.5 = (bf16[2,5,112,112]{3,2,1,0:T(8,128)(2,1)S(1)}, bf16[2,5,112,112]{3,2,1,0:T(8,128)(2,1)S(1)}, u32[]{:S(2)}, u32[]{:S(2)}) collective-permute-start(bf16[2,5,112,112]{3,2,1,0:T(8,128)(2,1)S(1)} %shard_map.75), channel_id=1, source_target_pairs={{0,8},{4,12},{1,9},{5,13},{2,10},{6,14},{3,11},{7,15},{16,24},{20,... | collective-permute-start | bytes 752648 | tf_op jit(solution)/shard_map/ppermute | solution.py:417
  60.7 1.0 collective-permute-done.29.rest_25_
  61.6 1.2 %collective-permute-start.15 = (bf16[144,1152]{1,0:T(8,128)(2,1)S(1)}, bf16[144,1152]{1,0:T(8,128)(2,1)}, u32[]{:S(2)}, u32[]{:S(2)}) collective-permute-start(bf16[144,1152]{1,0:T(8,128)(2,1)S(1)} %collective-permute-done.11.rest_7_), channel_id=1, source_target_pairs={{0,2},{1,3},{2,0},{3,1},{4,6},{5,7},{6,4},{7,5},{8,10},{9,11},{10,... | collective-permute-start | bytes 995336 | tf_op jit(solution)/shard_map/ppermute | solution.py:370
  62.9 0.5 collective-permute-done.27.rest_23_
  63.3 1.2 collective-permute-start.12
  64.6 0.7 collective-permute-start.31
  65.3 11.4 %collective-permute-done.5.rest_1_ = bf16[2,5,112,112]{3,2,1,0:T(8,128)(2,1)S(1)} collective-permute-done((bf16[2,5,112,112]{3,2,1,0:T(8,128)(2,1)S(1)}, bf16[2,5,112,112]{3,2,1,0:T(8,128)(2,1)S(1)}, u32[]{:S(2)}, u32[]{:S(2)}) %collective-permute-start.5) | collective-permute-done | bytes 250912 | tf_op jit(solution)/shard_map/ppermute | solution.py:417
  77.1 0.8 shard_map.76.rest_0_
  77.9 1.2 %collective-permute-start.7 = (bf16[2,5,112,112]{3,2,1,0:T(8,128)(2,1)S(1)}, bf16[2,5,112,112]{3,2,1,0:T(8,128)(2,1)}, u32[]{:S(2)}, u32[]{:S(2)}) collective-permute-start(bf16[2,5,112,112]{3,2,1,0:T(8,128)(2,1)S(1)} %shard_map.76.rest_0_), channel_id=1, source_target_pairs={{0,2},{1,3},{2,0},{3,1},{4,6},{5,7},{6,4},{7,5},{8,10},{9,11},{10,... | collective-permute-start | bytes 752648 | tf_op jit(solution)/shard_map/ppermute | solution.py:430
  79.1 0.8 copy-done.31
  80.2 0.7 copy-done.33
  81.5 0.8 copy-done.35
  82.4 4.0 %collective-permute-done.7.rest_2_ = bf16[2,5,112,112]{3,2,1,0:T(8,128)(2,1)} collective-permute-done((bf16[2,5,112,112]{3,2,1,0:T(8,128)(2,1)S(1)}, bf16[2,5,112,112]{3,2,1,0:T(8,128)(2,1)}, u32[]{:S(2)}, u32[]{:S(2)}) %collective-permute-start.7) | collective-permute-done | bytes 250912 | tf_op jit(solution)/shard_map/ppermute | solution.py:430
  86.4 1.0 collective-permute-start.8
  87.5 1.4 %collective-permute-done.8.rest_3_ = bf16[2,5,112,112]{3,2,1,0:T(8,128)(2,1)} collective-permute-done((bf16[2,5,112,112]{3,2,1,0:T(8,128)(2,1)}, bf16[2,5,112,112]{3,2,1,0:T(8,128)(2,1)}, u32[]{:S(2)}, u32[]{:S(2)}) %collective-permute-start.8) | collective-permute-done | bytes 250912 | tf_op jit(solution)/shard_map/ppermute | solution.py:433
  89.0 1.6 %copy-done.4 = bf16[2,2,128,2240]{2,3,1,0:T(8,128)(2,1)S(1)} copy-done((bf16[2,2,128,2240]{2,3,1,0:T(8,128)(2,1)S(1)}, bf16[2,2,128,2240]{2,3,1,0:T(8,128)(2,1)}, u32[]{:S(2)}) %copy-start.4) | copy-done | bytes 2293784
  90.6 1.0 copy-done.6
  91.6 1.0 copy-done.8
  92.6 1.0 copy-done.10
  93.5 1.0 copy-done.12
  94.5 1.0 copy-done.14
  95.5 1.0 copy-done.16
  96.5 1.0 copy-done.18
  97.4 1.0 copy-done.20
  98.4 1.0 copy-done.22
  99.4 1.0 copy-done.24
  100.4 1.0 copy-done.26
  101.3 1.0 copy-done.28
  102.3 1.0 copy-done.30
  103.3 1.0 copy-done.32
  104.3 1.0 copy-done.34
  105.2 1.0 copy-done.36
  106.2 11.1 %project.1 = bf16[2,2,2240,128]{3,2,1,0:T(8,128)(2,1)} custom-call(bf16[2,2,2240,128]{3,2,1,0:T(8,128)(2,1)S(1)} %bitcast.4, f32[20,112]{1,0:T(8,128)S(1)} %reshape.3.gain_ref, bf16[2,5,112,112]{3,2,1,0:T(8,128)(2,1)S(1)} %shard_map.76.rest_0_, bf16[2,5,112,112]{3,2,1,0:T(8,128)(2,1)} %collective-permute-done.6.rest_1_, ...), custom_call_target="tpu_custom_call" | custom-call | flops 6165626880 | bytes 14622720 | tf_op jit(solution)/shard_map/project/pallas_call | solution.py:309
  (87 shorter events, 2.6 us)
Async XLA Ops:
  2.1 10.6 %collective-permute-start.17 = (bf16[144,1152]{1,0:T(8,128)(2,1)S(1)}, bf16[144,1152]{1,0:T(8,128)(2,1)S(1)}, u32[]{:S(2)}, u32[]{:S(2)}) collective-permute-start(bf16[144,1152]{1,0:T(8,128)(2,1)S(1)} %dynamic-slice_select_fusion), channel_id=1, source_target_pairs={{0,12},{4,0},{8,4},{12,8},{1,13},{5,1},{9,5},{13,9},{2,14},{6,2},{... | collective-permute-start | bytes 995336 | tf_op jit(solution)/shard_map/ppermute | solution.py:360
  2.3 19.7 %copy-start.3 = (s32[2]{0:T(128)S(1)}, s32[2]{0:T(128)}, u32[]{:S(2)}) copy-start(s32[2]{0:T(128)} %blocks.5) | copy-start | bytes 28
  2.3 38.8 %copy-start.2 = (s32[2]{0:T(128)S(1)}, s32[2]{0:T(128)}, u32[]{:S(2)}) copy-start(s32[2]{0:T(128)} %flags.5) | copy-start | bytes 28
  6.8 15.2 %collective-permute-start.2 = (bf16[2,2,5,112,112]{4,3,2,1,0:T(8,128)(2,1)}, bf16[2,2,5,112,112]{4,3,2,1,0:T(8,128)(2,1)S(1)}, u32[]{:S(2)}, u32[]{:S(2)}) collective-permute-start(bf16[2,2,5,112,112]{4,3,2,1,0:T(8,128)(2,1)} %get-tuple-element.12), channel_id=1, source_target_pairs={{0,1},{1,0},{2,3},{3,2},{4,5},{5,4},{6,7},{7,6},{8,9},{9,8},{10,11... | collective-permute-start | bytes 1505288 | tf_op jit(solution)/shard_map/ppermute | solution.py:410
  7.8 12.9 %collective-permute-start.9 = (bf16[144,1152]{1,0:T(8,128)(2,1)S(1)}, bf16[144,1152]{1,0:T(8,128)(2,1)S(1)}, u32[]{:S(2)}, u32[]{:S(2)}) collective-permute-start(bf16[144,1152]{1,0:T(8,128)(2,1)S(1)} %dynamic-slice_select_fusion), channel_id=1, source_target_pairs={{0,4},{4,8},{8,12},{12,0},{1,5},{5,9},{9,13},{13,1},{2,6},{6,10},{... | collective-permute-start | bytes 995336 | tf_op jit(solution)/shard_map/ppermute | solution.py:360
  12.7 22.3 %collective-permute-start.21 = (bf16[144,1152]{1,0:T(8,128)(2,1)S(1)}, bf16[144,1152]{1,0:T(8,128)(2,1)S(1)}, u32[]{:S(2)}, u32[]{:S(2)}) collective-permute-start(bf16[144,1152]{1,0:T(8,128)(2,1)S(1)} %collective-permute-done.17.rest_13_), channel_id=1, source_target_pairs={{0,16},{16,0},{1,17},{17,1},{2,18},{18,2},{3,19},{19,3},{4,20},{20... | collective-permute-start | bytes 995336 | tf_op jit(solution)/shard_map/ppermute | solution.py:367
  13.9 21.3 %collective-permute-start.19 = (bf16[144,1152]{1,0:T(8,128)(2,1)S(1)}, bf16[144,1152]{1,0:T(8,128)(2,1)S(1)}, u32[]{:S(2)}, u32[]{:S(2)}) collective-permute-start(bf16[144,1152]{1,0:T(8,128)(2,1)S(1)} %collective-permute-done.17.rest_13_), channel_id=1, source_target_pairs={{0,2},{1,3},{2,0},{3,1},{4,6},{5,7},{6,4},{7,5},{8,10},{9,11},{10,... | collective-permute-start | bytes 995336 | tf_op jit(solution)/shard_map/ppermute | solution.py:370
  15.1 21.4 %collective-permute-start.18 = (bf16[144,1152]{1,0:T(8,128)(2,1)S(1)}, bf16[144,1152]{1,0:T(8,128)(2,1)S(1)}, u32[]{:S(2)}, u32[]{:S(2)}) collective-permute-start(bf16[144,1152]{1,0:T(8,128)(2,1)S(1)} %collective-permute-done.17.rest_13_), channel_id=1, source_target_pairs={{0,1},{1,0},{2,3},{3,2},{4,5},{5,4},{6,7},{7,6},{8,9},{9,8},{10,11... | collective-permute-start | bytes 995336 | tf_op jit(solution)/shard_map/ppermute | solution.py:373
  20.8 20.0 %collective-permute-start.25 = (bf16[144,1152]{1,0:T(8,128)(2,1)S(1)}, bf16[144,1152]{1,0:T(8,128)(2,1)S(1)}, u32[]{:S(2)}, u32[]{:S(2)}) collective-permute-start(bf16[144,1152]{1,0:T(8,128)(2,1)S(1)} %collective-permute-done.9.rest_5_), channel_id=1, source_target_pairs={{0,4},{4,8},{8,12},{12,0},{1,5},{5,9},{9,13},{13,1},{2,6},{6,10},{... | collective-permute-start | bytes 995336 | tf_op jit(solution)/shard_map/ppermute | solution.py:360
  22.0 7.4 %collective-permute-start.1 = (s32[2]{0:T(128)S(1)}, s32[2]{0:T(128)S(1)}, u32[]{:S(2)}, u32[]{:S(2)}) collective-permute-start(s32[2]{0:T(128)S(1)} %copy-done.3), channel_id=1, source_target_pairs={{0,8},{4,12},{1,9},{5,13},{2,10},{6,14},{3,11},{7,15},{16,24},{20,... | collective-permute-start | bytes 32 | tf_op jit(solution)/shard_map/ppermute | solution.py:426
  23.3 1.3 %copy-start = (f32[2,2,5,112,112]{4,3,2,1,0:T(8,128)S(1)}, f32[2,2,5,112,112]{4,3,2,1,0:T(8,128)}, u32[]{:S(2)}) copy-start(f32[2,2,5,112,112]{4,3,2,1,0:T(8,128)} %get-tuple-element.11.own_ref) | copy-start | bytes 3010564
  24.6 62.9 %copy-start.37 = (f32[2240]{0:T(1024)S(1)}, f32[2240]{0:T(1024)}, u32[]{:S(2)}) copy-start(f32[2240]{0:T(1024)} %param.13) | copy-start | bytes 26884
  24.6 64.4 %copy-start.1 = (bf16[560,2240]{1,0:T(8,128)(2,1)S(1)}, bf16[560,2240]{1,0:T(8,128)(2,1)}, u32[]{:S(2)}) copy-start(bf16[560,2240]{1,0:T(8,128)(2,1)} %rest_4_.1) | copy-start | bytes 7526404
  29.4 4.3 %collective-permute-start = (s32[2]{0:T(128)S(1)}, s32[2]{0:T(128)S(1)}, u32[]{:S(2)}, u32[]{:S(2)}) collective-permute-start(s32[2]{0:T(128)S(1)} %copy-done.3), channel_id=1, source_target_pairs={{0,4},{4,8},{8,12},{1,5},{5,9},{9,13},{2,6},{6,10},{10,14},{3,7},{... | collective-permute-start | bytes 32 | tf_op jit(solution)/shard_map/ppermute | solution.py:412
  33.8 7.1 %collective-permute-start.3 = (bf16[2,5,112,112]{3,2,1,0:T(8,128)(2,1)S(1)}, bf16[2,5,112,112]{3,2,1,0:T(8,128)(2,1)S(1)}, u32[]{:S(2)}, u32[]{:S(2)}) collective-permute-start(bf16[2,5,112,112]{3,2,1,0:T(8,128)(2,1)S(1)} %get-tuple-element.14), channel_id=1, source_target_pairs={{0,2},{1,3},{2,0},{3,1},{4,6},{5,7},{6,4},{7,5},{8,10},{9,11},{10,... | collective-permute-start | bytes 752648 | tf_op jit(solution)/shard_map/ppermute | solution.py:411
  35.0 51.4 %copy-start.5 = (bf16[144,1152]{1,0:T(8,128)(2,1)}, bf16[144,1152]{1,0:T(8,128)(2,1)S(1)}, u32[]{:S(2)}) copy-start(bf16[144,1152]{1,0:T(8,128)(2,1)S(1)} %collective-permute-done.21.rest_17_) | copy-start | bytes 995332
  35.0 11.5 %collective-permute-start.13 = (bf16[144,1152]{1,0:T(8,128)(2,1)S(1)}, bf16[144,1152]{1,0:T(8,128)(2,1)S(1)}, u32[]{:S(2)}, u32[]{:S(2)}) collective-permute-start(bf16[144,1152]{1,0:T(8,128)(2,1)S(1)} %collective-permute-done.9.rest_5_), channel_id=1, source_target_pairs={{0,2},{1,3},{2,0},{3,1},{4,6},{5,7},{6,4},{7,5},{8,10},{9,11},{10,... | collective-permute-start | bytes 995336 | tf_op jit(solution)/shard_map/ppermute | solution.py:370
  35.2 51.1 %copy-start.7 = (bf16[144,1152]{1,0:T(8,128)(2,1)}, bf16[144,1152]{1,0:T(8,128)(2,1)S(1)}, u32[]{:S(2)}) copy-start(bf16[144,1152]{1,0:T(8,128)(2,1)S(1)} %collective-permute-done.19.rest_15_) | copy-start | bytes 995332
  35.2 12.6 %collective-permute-start.11 = (bf16[144,1152]{1,0:T(8,128)(2,1)S(1)}, bf16[144,1152]{1,0:T(8,128)(2,1)S(1)}, u32[]{:S(2)}, u32[]{:S(2)}) collective-permute-start(bf16[144,1152]{1,0:T(8,128)(2,1)S(1)} %collective-permute-done.9.rest_5_), channel_id=1, source_target_pairs={{0,16},{16,0},{1,17},{17,1},{2,18},{18,2},{3,19},{19,3},{4,20},{20... | collective-permute-start | bytes 995336 | tf_op jit(solution)/shard_map/ppermute | solution.py:367
  37.2 14.3 %collective-permute-start.10 = (bf16[144,1152]{1,0:T(8,128)(2,1)S(1)}, bf16[144,1152]{1,0:T(8,128)(2,1)S(1)}, u32[]{:S(2)}, u32[]{:S(2)}) collective-permute-start(bf16[144,1152]{1,0:T(8,128)(2,1)S(1)} %collective-permute-done.9.rest_5_), channel_id=1, source_target_pairs={{0,1},{1,0},{2,3},{3,2},{4,5},{5,4},{6,7},{7,6},{8,9},{9,8},{10,11... | collective-permute-start | bytes 995336 | tf_op jit(solution)/shard_map/ppermute | solution.py:373
  40.8 45.6 %copy-start.11 = (bf16[144,1152]{1,0:T(8,128)(2,1)}, bf16[144,1152]{1,0:T(8,128)(2,1)S(1)}, u32[]{:S(2)}) copy-start(bf16[144,1152]{1,0:T(8,128)(2,1)S(1)} %collective-permute-done.25.rest_21_) | copy-start | bytes 995332
  40.8 12.7 %collective-permute-start.22 = (bf16[144,1152]{1,0:T(8,128)(2,1)S(1)}, bf16[144,1152]{1,0:T(8,128)(2,1)S(1)}, u32[]{:S(2)}, u32[]{:S(2)}) collective-permute-start(bf16[144,1152]{1,0:T(8,128)(2,1)S(1)} %collective-permute-done.21.rest_17_), channel_id=1, source_target_pairs={{0,1},{1,0},{2,3},{3,2},{4,5},{5,4},{6,7},{7,6},{8,9},{9,8},{10,11... | collective-permute-start | bytes 995336 | tf_op jit(solution)/shard_map/ppermute | solution.py:373
  40.9 14.5 %collective-permute-start.23 = (bf16[144,1152]{1,0:T(8,128)(2,1)S(1)}, bf16[144,1152]{1,0:T(8,128)(2,1)S(1)}, u32[]{:S(2)}, u32[]{:S(2)}) collective-permute-start(bf16[144,1152]{1,0:T(8,128)(2,1)S(1)} %collective-permute-done.19.rest_15_), channel_id=1, source_target_pairs={{0,16},{16,0},{1,17},{17,1},{2,18},{18,2},{3,19},{19,3},{4,20},{20... | collective-permute-start | bytes 995336 | tf_op jit(solution)/shard_map/ppermute | solution.py:367
  46.5 39.9 %copy-start.13 = (bf16[144,1152]{1,0:T(8,128)(2,1)}, bf16[144,1152]{1,0:T(8,128)(2,1)S(1)}, u32[]{:S(2)}) copy-start(bf16[144,1152]{1,0:T(8,128)(2,1)S(1)} %collective-permute-done.13.rest_9_) | copy-start | bytes 995332
  46.5 9.5 %collective-permute-start.4 = (bf16[2,5,112,112]{3,2,1,0:T(8,128)(2,1)S(1)}, bf16[2,5,112,112]{3,2,1,0:T(8,128)(2,1)S(1)}, u32[]{:S(2)}, u32[]{:S(2)}) collective-permute-start(bf16[2,5,112,112]{3,2,1,0:T(8,128)(2,1)S(1)} %get-tuple-element.16), channel_id=1, source_target_pairs={{0,4},{4,8},{8,12},{1,5},{5,9},{9,13},{2,6},{6,10},{10,14},{3,7},{... | collective-permute-start | bytes 752648 | tf_op jit(solution)/shard_map/ppermute | solution.py:417
  47.8 38.6 %copy-start.15 = (bf16[144,1152]{1,0:T(8,128)(2,1)}, bf16[144,1152]{1,0:T(8,128)(2,1)S(1)}, u32[]{:S(2)}) copy-start(bf16[144,1152]{1,0:T(8,128)(2,1)S(1)} %collective-permute-done.11.rest_7_) | copy-start | bytes 995332
  47.8 11.5 %collective-permute-start.20 = (bf16[144,1152]{1,0:T(8,128)(2,1)S(1)}, bf16[144,1152]{1,0:T(8,128)(2,1)S(1)}, u32[]{:S(2)}, u32[]{:S(2)}) collective-permute-start(bf16[144,1152]{1,0:T(8,128)(2,1)S(1)} %collective-permute-done.19.rest_15_), channel_id=1, source_target_pairs={{0,1},{1,0},{2,3},{3,2},{4,5},{5,4},{6,7},{7,6},{8,9},{9,8},{10,11... | collective-permute-start | bytes 995336 | tf_op jit(solution)/shard_map/ppermute | solution.py:373
  52.2 9.4 %collective-permute-start.29 = (bf16[144,1152]{1,0:T(8,128)(2,1)S(1)}, bf16[144,1152]{1,0:T(8,128)(2,1)S(1)}, u32[]{:S(2)}, u32[]{:S(2)}) collective-permute-start(bf16[144,1152]{1,0:T(8,128)(2,1)S(1)} %collective-permute-done.25.rest_21_), channel_id=1, source_target_pairs={{0,16},{16,0},{1,17},{17,1},{2,18},{18,2},{3,19},{19,3},{4,20},{20... | collective-permute-start | bytes 995336 | tf_op jit(solution)/shard_map/ppermute | solution.py:367
  54.2 9.2 %collective-permute-start.27 = (bf16[144,1152]{1,0:T(8,128)(2,1)S(1)}, bf16[144,1152]{1,0:T(8,128)(2,1)}, u32[]{:S(2)}, u32[]{:S(2)}) collective-permute-start(bf16[144,1152]{1,0:T(8,128)(2,1)S(1)} %collective-permute-done.25.rest_21_), channel_id=1, source_target_pairs={{0,2},{1,3},{2,0},{3,1},{4,6},{5,7},{6,4},{7,5},{8,10},{9,11},{10,... | collective-permute-start | bytes 995336 | tf_op jit(solution)/shard_map/ppermute | solution.py:370
  55.4 31.0 %copy-start.21 = (bf16[144,1152]{1,0:T(8,128)(2,1)}, bf16[144,1152]{1,0:T(8,128)(2,1)S(1)}, u32[]{:S(2)}) copy-start(bf16[144,1152]{1,0:T(8,128)(2,1)S(1)} %collective-permute-done.23.rest_19_) | copy-start | bytes 995332
  55.4 9.1 %collective-permute-start.26 = (bf16[144,1152]{1,0:T(8,128)(2,1)S(1)}, bf16[144,1152]{1,0:T(8,128)(2,1)S(1)}, u32[]{:S(2)}, u32[]{:S(2)}) collective-permute-start(bf16[144,1152]{1,0:T(8,128)(2,1)S(1)} %collective-permute-done.25.rest_21_), channel_id=1, source_target_pairs={{0,1},{1,0},{2,3},{3,2},{4,5},{5,4},{6,7},{7,6},{8,9},{9,8},{10,11... | collective-permute-start | bytes 995336 | tf_op jit(solution)/shard_map/ppermute | solution.py:373
  56.0 8.6 %collective-permute-start.14 = (bf16[144,1152]{1,0:T(8,128)(2,1)S(1)}, bf16[144,1152]{1,0:T(8,128)(2,1)S(1)}, u32[]{:S(2)}, u32[]{:S(2)}) collective-permute-start(bf16[144,1152]{1,0:T(8,128)(2,1)S(1)} %collective-permute-done.13.rest_9_), channel_id=1, source_target_pairs={{0,1},{1,0},{2,3},{3,2},{4,5},{5,4},{6,7},{7,6},{8,9},{9,8},{10,11... | collective-permute-start | bytes 995336 | tf_op jit(solution)/shard_map/ppermute | solution.py:373
  59.3 27.0 %copy-start.23 = (bf16[144,1152]{1,0:T(8,128)(2,1)}, bf16[144,1152]{1,0:T(8,128)(2,1)S(1)}, u32[]{:S(2)}) copy-start(bf16[144,1152]{1,0:T(8,128)(2,1)S(1)} %collective-permute-done.20.rest_16_) | copy-start | bytes 995332
  59.4 17.3 %collective-permute-start.5 = (bf16[2,5,112,112]{3,2,1,0:T(8,128)(2,1)S(1)}, bf16[2,5,112,112]{3,2,1,0:T(8,128)(2,1)S(1)}, u32[]{:S(2)}, u32[]{:S(2)}) collective-permute-start(bf16[2,5,112,112]{3,2,1,0:T(8,128)(2,1)S(1)} %shard_map.75), channel_id=1, source_target_pairs={{0,8},{4,12},{1,9},{5,13},{2,10},{6,14},{3,11},{7,15},{16,24},{20,... | collective-permute-start | bytes 752648 | tf_op jit(solution)/shard_map/ppermute | solution.py:417
  61.6 24.8 %copy-start.25 = (bf16[144,1152]{1,0:T(8,128)(2,1)}, bf16[144,1152]{1,0:T(8,128)(2,1)S(1)}, u32[]{:S(2)}) copy-start(bf16[144,1152]{1,0:T(8,128)(2,1)S(1)} %collective-permute-done.29.rest_25_) | copy-start | bytes 995332
  61.6 16.2 %collective-permute-start.15 = (bf16[144,1152]{1,0:T(8,128)(2,1)S(1)}, bf16[144,1152]{1,0:T(8,128)(2,1)}, u32[]{:S(2)}, u32[]{:S(2)}) collective-permute-start(bf16[144,1152]{1,0:T(8,128)(2,1)S(1)} %collective-permute-done.11.rest_7_), channel_id=1, source_target_pairs={{0,2},{1,3},{2,0},{3,1},{4,6},{5,7},{6,4},{7,5},{8,10},{9,11},{10,... | collective-permute-start | bytes 995336 | tf_op jit(solution)/shard_map/ppermute | solution.py:370
  63.3 15.8 %collective-permute-start.12 = (bf16[144,1152]{1,0:T(8,128)(2,1)S(1)}, bf16[144,1152]{1,0:T(8,128)(2,1)S(1)}, u32[]{:S(2)}, u32[]{:S(2)}) collective-permute-start(bf16[144,1152]{1,0:T(8,128)(2,1)S(1)} %collective-permute-done.11.rest_7_), channel_id=1, source_target_pairs={{0,1},{1,0},{2,3},{3,2},{4,5},{5,4},{6,7},{7,6},{8,9},{9,8},{10,11... | collective-permute-start | bytes 995336 | tf_op jit(solution)/shard_map/ppermute | solution.py:373
  64.5 21.9 %copy-start.27 = (bf16[144,1152]{1,0:T(8,128)(2,1)}, bf16[144,1152]{1,0:T(8,128)(2,1)S(1)}, u32[]{:S(2)}) copy-start(bf16[144,1152]{1,0:T(8,128)(2,1)S(1)} %collective-permute-done.26.rest_22_) | copy-start | bytes 995332
  64.5 15.7 %collective-permute-start.24 = (bf16[144,1152]{1,0:T(8,128)(2,1)S(1)}, bf16[144,1152]{1,0:T(8,128)(2,1)S(1)}, u32[]{:S(2)}, u32[]{:S(2)}) collective-permute-start(bf16[144,1152]{1,0:T(8,128)(2,1)S(1)} %collective-permute-done.23.rest_19_), channel_id=1, source_target_pairs={{0,1},{1,0},{2,3},{3,2},{4,5},{5,4},{6,7},{7,6},{8,9},{9,8},{10,11... | collective-permute-start | bytes 995336 | tf_op jit(solution)/shard_map/ppermute | solution.py:373
  64.6 21.8 %copy-start.29 = (bf16[144,1152]{1,0:T(8,128)(2,1)}, bf16[144,1152]{1,0:T(8,128)(2,1)S(1)}, u32[]{:S(2)}) copy-start(bf16[144,1152]{1,0:T(8,128)(2,1)S(1)} %collective-permute-done.14.rest_10_) | copy-start | bytes 995332
  64.6 16.5 %collective-permute-start.31 = (bf16[144,1152]{1,0:T(8,128)(2,1)}, bf16[144,1152]{1,0:T(8,128)(2,1)}, u32[]{:S(2)}, u32[]{:S(2)}) collective-permute-start(bf16[144,1152]{1,0:T(8,128)(2,1)} %collective-permute-done.27.rest_23_), channel_id=1, source_target_pairs={{0,16},{16,0},{1,17},{17,1},{2,18},{18,2},{3,19},{19,3},{4,20},{20... | collective-permute-start | bytes 995336 | tf_op jit(solution)/shard_map/ppermute | solution.py:367
  76.6 4.8 %collective-permute-start.30 = (bf16[144,1152]{1,0:T(8,128)(2,1)S(1)}, bf16[144,1152]{1,0:T(8,128)(2,1)S(1)}, u32[]{:S(2)}, u32[]{:S(2)}) collective-permute-start(bf16[144,1152]{1,0:T(8,128)(2,1)S(1)} %collective-permute-done.29.rest_25_), channel_id=1, source_target_pairs={{0,1},{1,0},{2,3},{3,2},{4,5},{5,4},{6,7},{7,6},{8,9},{9,8},{10,11... | collective-permute-start | bytes 995336 | tf_op jit(solution)/shard_map/ppermute | solution.py:373
  77.9 8.5 %collective-permute-start.7 = (bf16[2,5,112,112]{3,2,1,0:T(8,128)(2,1)S(1)}, bf16[2,5,112,112]{3,2,1,0:T(8,128)(2,1)}, u32[]{:S(2)}, u32[]{:S(2)}) collective-permute-start(bf16[2,5,112,112]{3,2,1,0:T(8,128)(2,1)S(1)} %shard_map.76.rest_0_), channel_id=1, source_target_pairs={{0,2},{1,3},{2,0},{3,1},{4,6},{5,7},{6,4},{7,5},{8,10},{9,11},{10,... | collective-permute-start | bytes 752648 | tf_op jit(solution)/shard_map/ppermute | solution.py:430
  79.9 7.6 %collective-permute-start.28 = (bf16[144,1152]{1,0:T(8,128)(2,1)}, bf16[144,1152]{1,0:T(8,128)(2,1)}, u32[]{:S(2)}, u32[]{:S(2)}) collective-permute-start(bf16[144,1152]{1,0:T(8,128)(2,1)} %collective-permute-done.27.rest_23_), channel_id=1, source_target_pairs={{0,1},{1,0},{2,3},{3,2},{4,5},{5,4},{6,7},{7,6},{8,9},{9,8},{10,11... | collective-permute-start | bytes 995336 | tf_op jit(solution)/shard_map/ppermute | solution.py:373
  81.0 6.6 %collective-permute-start.16 = (bf16[144,1152]{1,0:T(8,128)(2,1)}, bf16[144,1152]{1,0:T(8,128)(2,1)}, u32[]{:S(2)}, u32[]{:S(2)}) collective-permute-start(bf16[144,1152]{1,0:T(8,128)(2,1)} %collective-permute-done.15.rest_11_), channel_id=1, source_target_pairs={{0,1},{1,0},{2,3},{3,2},{4,5},{5,4},{6,7},{7,6},{8,9},{9,8},{10,11... | collective-permute-start | bytes 995336 | tf_op jit(solution)/shard_map/ppermute | solution.py:373
  81.1 6.4 %collective-permute-start.32 = (bf16[144,1152]{1,0:T(8,128)(2,1)}, bf16[144,1152]{1,0:T(8,128)(2,1)}, u32[]{:S(2)}, u32[]{:S(2)}) collective-permute-start(bf16[144,1152]{1,0:T(8,128)(2,1)} %collective-permute-done.31.rest_27_), channel_id=1, source_target_pairs={{0,1},{1,0},{2,3},{3,2},{4,5},{5,4},{6,7},{7,6},{8,9},{9,8},{10,11... | collective-permute-start | bytes 995336 | tf_op jit(solution)/shard_map/ppermute | solution.py:373
  82.2 5.3 %collective-permute-start.6 = (bf16[2,5,112,112]{3,2,1,0:T(8,128)(2,1)S(1)}, bf16[2,5,112,112]{3,2,1,0:T(8,128)(2,1)}, u32[]{:S(2)}, u32[]{:S(2)}) collective-permute-start(bf16[2,5,112,112]{3,2,1,0:T(8,128)(2,1)S(1)} %shard_map.76.rest_0_), channel_id=1, source_target_pairs={{0,1},{1,0},{2,3},{3,2},{4,5},{5,4},{6,7},{7,6},{8,9},{9,8},{10,11... | collective-permute-start | bytes 752648 | tf_op jit(solution)/shard_map/ppermute | solution.py:433
  86.4 2.5 %collective-permute-start.8 = (bf16[2,5,112,112]{3,2,1,0:T(8,128)(2,1)}, bf16[2,5,112,112]{3,2,1,0:T(8,128)(2,1)}, u32[]{:S(2)}, u32[]{:S(2)}) collective-permute-start(bf16[2,5,112,112]{3,2,1,0:T(8,128)(2,1)} %collective-permute-done.7.rest_2_), channel_id=1, source_target_pairs={{0,1},{1,0},{2,3},{3,2},{4,5},{5,4},{6,7},{7,6},{8,9},{9,8},{10,11... | collective-permute-start | bytes 752648 | tf_op jit(solution)/shard_map/ppermute | solution.py:433
  89.0 1.6 %copy-start.4 = (bf16[2,2,128,2240]{2,3,1,0:T(8,128)(2,1)S(1)}, bf16[2,2,128,2240]{2,3,1,0:T(8,128)(2,1)}, u32[]{:S(2)}) copy-start(bf16[2,2,128,2240]{2,3,1,0:T(8,128)(2,1)} %param.7) | copy-start | bytes 6881284
  90.6 1.0 copy-start.6
  91.6 1.0 copy-start.8
  92.6 1.0 copy-start.10
  93.5 1.0 copy-start.12
  94.5 1.0 copy-start.14
  95.5 1.0 copy-start.16
  96.5 1.0 copy-start.18
  97.4 1.0 copy-start.20
  98.4 1.0 copy-start.22
  99.4 1.0 copy-start.24
  100.4 1.0 copy-start.26
  101.3 1.0 copy-start.28
  103.3 1.0 copy-start.32
  104.3 1.0 copy-start.34
  105.2 1.0 copy-start.36
  (7 other events, 5.4 us)

commit v2 on v1

--- a/solution.py
+++ b/solution.py
@@ -13,7 +13,8 @@
 
 norm_eps = 1e-06
 
-STATES_VMEM = 64843328
+STATES_VMEM = 63500000
+CUT_VMEM = 63500000
 SMALL_VMEM = 8 << 20
 PROJECT_VMEM = 36 << 20
 LANES = 128
@@ -330,9 +331,48 @@
     )(queries, gain, *states, *weights)
 
 
+def cut_kernel(chips, members, weight_ref, piece_ref, lines, sem):
+    row = lax.axis_index("row")
+    number = lax.axis_index("grp") * chips + row // 2
+    count, half = piece_ref.shape
+    over = members * count - weight_ref.shape[0]
+    start = pl.multiple_of(number * count - (number + 1) // members * over, 16)
+    copy = pltpu.make_async_copy(weight_ref.at[pl.ds(start, count)], lines, sem)
+    copy.start()
+    copy.wait()
+
+    @pl.when(lax.rem(row, 2) == 0)
+    def _():
+        piece_ref[...] = lines[:, :half]
+
+    @pl.when(lax.rem(row, 2) == 1)
+    def _():
+        rest = lines.shape[1] - half
+        full = rest // LANES * LANES
+        piece_ref[:, :full] = lines[:, half : half + full]
+        if full < half:
+            blank = jnp.zeros((count, half - rest), lines.dtype)
+            piece_ref[:, full:] = jnp.concatenate([lines[:, half + full :], blank], axis=1)
+
+
+def cut_piece(weight, groups, chips, piece_rows, half):
+    return pl.pallas_call(
+        functools.partial(cut_kernel, chips, groups * chips),
+        in_specs=[pl.BlockSpec(memory_space=pl.ANY)],
+        out_specs=pl.BlockSpec(memory_space=pltpu.VMEM),
+        out_shape=jax.ShapeDtypeStruct((piece_rows, half), weight.dtype),
+        scratch_shapes=[
+            pltpu.VMEM((piece_rows, weight.shape[1]), weight.dtype),
+            pltpu.SemaphoreType.DMA,
+        ],
+        compiler_params=pltpu.CompilerParams(vmem_limit_bytes=CUT_VMEM),
+        name="cut",
+    )(weight)
+
+
 def gather_weight(weight, sizes, places):
     groups, frms, rows = sizes
-    grp, _, row = places
+    grp, frm, row = places
     own_rows, width = weight.shape
     chips = rows // 2
     members = groups * chips
@@ -344,13 +384,9 @@
 
     def first_row(number):
         over = members * piece_rows - own_rows
-        assert over < piece_rows
         return number * piece_rows - (number + 1) // members * over
 
-    start = first_row(grp * chips + row // 2)
-    lines = lax.dynamic_slice_in_dim(weight, start, piece_rows, 0)
-    right = jnp.pad(lines[:, half:], ((0, 0), (0, 2 * half - width)))
-    piece = jnp.where(row % 2 == 0, lines[:, :half], right)
+    piece = cut_piece(weight, groups, chips, piece_rows, half)
     arrays, plan, reached = [weight], [], {}
     cores = [(i, i ^ 1) for i in range(rows)]
     order = sorted(range(1, frms), key=lambda s: min(s, frms - s))

time: 118 us -> 118 us (level)
  Pallas kernels: 17.8 us -> 19.6 us
    pallas_call x0 -> x1, Pallas kernels: none -> 1.84 us  [cut_piece(): pl.pallas_call(functools.partial(cut_kernel, chips, groups * chips), in_s...]
    unnamed x76 -> x78, local copies, waits for them, and re-layouts: 23 us -> 23 us
where the time goes in v2:
time: 118 us; the launch traced here: 117 us
  starting transfers between devices  38.9 us (33%)
  waiting for transfers between devices  35.4 us (30%)
  local copies, waits for them, and re-layouts  23 us (19%)
  Pallas kernels  19.6 us (17%)
    unnamed x78, local copies, waits for them, and re-layouts  23 us
    ppermute x12, starting transfers between devices, gather_weight(): arrays.append(lax.ppermute(block, 'row', cores))  16.3 us
    ppermute x2, waiting for transfers between devices, attention(): got = lax.ppermute(carry, 'frm', ahead(reach))  11.4 us
    pallas_call x1, Pallas kernels, project(): pl.pallas_call(functools.partial(project_kernel, chunks, pieces, table_of...  11 us
    ppermute x4, waiting for transfers between devices, gather_weight(): held[dg, dx + s] = lax.ppermute(block, 'row', ring(rows, 2 * s))  5.2 us
    ppermute x1, waiting for transfers between devices, attention(): far = lax.ppermute(blocks, 'frm', ahead(reach))  4.98 us
    ppermute x5, starting transfers between devices, gather_weight(): held[dg + s, dx] = lax.ppermute(block, 'grp', ring(groups, s))  4.62 us
    pallas_call x1, Pallas kernels, partial_states(): pl.pallas_call(functools.partial(state_kernel, chips, heads_per), in_spec...  4.5 us
  transfers between devices with their start and end apart: 33, of which 10 were waited for; matrix products, arithmetic and copies ran while one was open for 0% of the time, Pallas kernels for 6%

profile of v2, /device:TPU:25, one launch (start us, length us, event | category | flops | bytes accessed | tf_op | source)
XLA Modules:
  0.0 117.2 jit_solution(15868863849891903730)
XLA Ops:
  0.0 1.8 %cut.1 = bf16[144,1152]{1,0:T(8,128)(2,1)} custom-call(bf16[560,2240]{1,0:T(8,128)(2,1)} %rest_4_.1), custom_call_target="tpu_custom_call" | custom-call | tf_op jit(solution)/shard_map/cut/pallas_call | solution.py:359
  2.1 4.5 %states.1 = (f32[2,2,5,112,112]{4,3,2,1,0:T(8,128)}, bf16[2,2,5,112,112]{4,3,2,1,0:T(8,128)(2,1)}) custom-call(bf16[2,2,2240,128]{3,2,1,0:T(8,128)(2,1)} %bitcast.5, bf16[2,2,2240,128]{3,2,1,0:T(8,128)(2,1)} %bitcast.6), custom_call_target="tpu_custom_call" | custom-call | flops 2055208960 | bytes 4587520 | tf_op jit(solution)/shard_map/states/pallas_call | solution.py:100
  6.6 1.0 collective-permute-start.2
  7.6 3.1 %collective-permute-start.9 = (bf16[144,1152]{1,0:T(8,128)(2,1)S(1)}, bf16[144,1152]{1,0:T(8,128)(2,1)S(1)}, u32[]{:S(2)}, u32[]{:S(2)}) collective-permute-start(bf16[144,1152]{1,0:T(8,128)(2,1)S(1)} %copy-done.37), channel_id=1, source_target_pairs={{0,4},{4,8},{8,12},{12,0},{1,5},{5,9},{9,13},{13,1},{2,6},{6,10},{... | collective-permute-start | bytes 995336 | tf_op jit(solution)/shard_map/ppermute | solution.py:396
  10.7 1.9 %collective-permute-done.17.rest_13_ = bf16[144,1152]{1,0:T(8,128)(2,1)S(1)} collective-permute-done((bf16[144,1152]{1,0:T(8,128)(2,1)}, bf16[144,1152]{1,0:T(8,128)(2,1)S(1)}, u32[]{:S(2)}, u32[]{:S(2)}) %collective-permute-start.17) | collective-permute-done | bytes 331808 | tf_op jit(solution)/shard_map/ppermute | solution.py:396
  12.6 1.2 %collective-permute-start.21 = (bf16[144,1152]{1,0:T(8,128)(2,1)S(1)}, bf16[144,1152]{1,0:T(8,128)(2,1)S(1)}, u32[]{:S(2)}, u32[]{:S(2)}) collective-permute-start(bf16[144,1152]{1,0:T(8,128)(2,1)S(1)} %collective-permute-done.17.rest_13_), channel_id=1, source_target_pairs={{0,16},{16,0},{1,17},{17,1},{2,18},{18,2},{3,19},{19,3},{4,20},{20... | collective-permute-start | bytes 995336 | tf_op jit(solution)/shard_map/ppermute | solution.py:403
  13.9 1.2 %collective-permute-start.19 = (bf16[144,1152]{1,0:T(8,128)(2,1)S(1)}, bf16[144,1152]{1,0:T(8,128)(2,1)S(1)}, u32[]{:S(2)}, u32[]{:S(2)}) collective-permute-start(bf16[144,1152]{1,0:T(8,128)(2,1)S(1)} %collective-permute-done.17.rest_13_), channel_id=1, source_target_pairs={{0,2},{1,3},{2,0},{3,1},{4,6},{5,7},{6,4},{7,5},{8,10},{9,11},{10,... | collective-permute-start | bytes 995336 | tf_op jit(solution)/shard_map/ppermute | solution.py:406
  15.1 3.2 %collective-permute-start.18 = (bf16[144,1152]{1,0:T(8,128)(2,1)S(1)}, bf16[144,1152]{1,0:T(8,128)(2,1)S(1)}, u32[]{:S(2)}, u32[]{:S(2)}) collective-permute-start(bf16[144,1152]{1,0:T(8,128)(2,1)S(1)} %collective-permute-done.17.rest_13_), channel_id=1, source_target_pairs={{0,1},{1,0},{2,3},{3,2},{4,5},{5,4},{6,7},{7,6},{8,9},{9,8},{10,11... | collective-permute-start | bytes 995336 | tf_op jit(solution)/shard_map/ppermute | solution.py:409
  18.3 2.4 %collective-permute-done.9.rest_5_ = bf16[144,1152]{1,0:T(8,128)(2,1)S(1)} collective-permute-done((bf16[144,1152]{1,0:T(8,128)(2,1)S(1)}, bf16[144,1152]{1,0:T(8,128)(2,1)S(1)}, u32[]{:S(2)}, u32[]{:S(2)}) %collective-permute-start.9) | collective-permute-done | bytes 331808 | tf_op jit(solution)/shard_map/ppermute | solution.py:396
  20.7 1.0 collective-permute-start.25
  21.8 1.3 %collective-permute-start.1 = (s32[2]{0:T(128)S(1)}, s32[2]{0:T(128)S(1)}, u32[]{:S(2)}, u32[]{:S(2)}) collective-permute-start(s32[2]{0:T(128)S(1)} %copy-done.3), channel_id=1, source_target_pairs={{0,8},{4,12},{1,9},{5,13},{2,10},{6,14},{3,11},{7,15},{16,24},{20,... | collective-permute-start | bytes 32 | tf_op jit(solution)/shard_map/ppermute | solution.py:462
  23.1 1.2 %copy-done.1 = f32[2,2,5,112,112]{4,3,2,1,0:T(8,128)S(1)} copy-done((f32[2,2,5,112,112]{4,3,2,1,0:T(8,128)S(1)}, f32[2,2,5,112,112]{4,3,2,1,0:T(8,128)}, u32[]{:S(2)}) %copy-start.1) | copy-done | bytes 1003544
  24.5 5.0 %collective-permute-done.1.far = s32[2]{0:T(128)S(1)} collective-permute-done((s32[2]{0:T(128)S(1)}, s32[2]{0:T(128)S(1)}, u32[]{:S(2)}, u32[]{:S(2)}) %collective-permute-start.1) | collective-permute-done | bytes 40 | tf_op jit(solution)/shard_map/ppermute | solution.py:462
  29.4 1.3 %collective-permute-start = (s32[2]{0:T(128)S(1)}, s32[2]{0:T(128)S(1)}, u32[]{:S(2)}, u32[]{:S(2)}) collective-permute-start(s32[2]{0:T(128)S(1)} %copy-done.3), channel_id=1, source_target_pairs={{0,4},{4,8},{8,12},{1,5},{5,9},{9,13},{2,6},{6,10},{10,14},{3,7},{... | collective-permute-start | bytes 32 | tf_op jit(solution)/shard_map/ppermute | solution.py:448
  30.7 3.0 %collective-permute-done.near.far = s32[2]{0:T(128)S(1)} collective-permute-done((s32[2]{0:T(128)S(1)}, s32[2]{0:T(128)S(1)}, u32[]{:S(2)}, u32[]{:S(2)}) %collective-permute-start) | collective-permute-done | bytes 40 | tf_op jit(solution)/shard_map/ppermute | solution.py:448
  33.7 1.2 %collective-permute-start.3 = (bf16[2,5,112,112]{3,2,1,0:T(8,128)(2,1)S(1)}, bf16[2,5,112,112]{3,2,1,0:T(8,128)(2,1)S(1)}, u32[]{:S(2)}, u32[]{:S(2)}) collective-permute-start(bf16[2,5,112,112]{3,2,1,0:T(8,128)(2,1)S(1)} %get-tuple-element.14), channel_id=1, source_target_pairs={{0,2},{1,3},{2,0},{3,1},{4,6},{5,7},{6,4},{7,5},{8,10},{9,11},{10,... | collective-permute-start | bytes 752648 | tf_op jit(solution)/shard_map/ppermute | solution.py:447
  35.2 1.2 %collective-permute-start.11 = (bf16[144,1152]{1,0:T(8,128)(2,1)S(1)}, bf16[144,1152]{1,0:T(8,128)(2,1)S(1)}, u32[]{:S(2)}, u32[]{:S(2)}) collective-permute-start(bf16[144,1152]{1,0:T(8,128)(2,1)S(1)} %collective-permute-done.9.rest_5_), channel_id=1, source_target_pairs={{0,16},{16,0},{1,17},{17,1},{2,18},{18,2},{3,19},{19,3},{4,20},{20... | collective-permute-start | bytes 995336 | tf_op jit(solution)/shard_map/ppermute | solution.py:403
  36.5 0.7 copy-done.9
  37.2 3.6 %collective-permute-start.10 = (bf16[144,1152]{1,0:T(8,128)(2,1)S(1)}, bf16[144,1152]{1,0:T(8,128)(2,1)S(1)}, u32[]{:S(2)}, u32[]{:S(2)}) collective-permute-start(bf16[144,1152]{1,0:T(8,128)(2,1)S(1)} %collective-permute-done.9.rest_5_), channel_id=1, source_target_pairs={{0,1},{1,0},{2,3},{3,2},{4,5},{5,4},{6,7},{7,6},{8,9},{9,8},{10,11... | collective-permute-start | bytes 995336 | tf_op jit(solution)/shard_map/ppermute | solution.py:409
  41.1 0.7 shard_map.74
  41.8 4.7 %collective-permute-done.13.rest_9_ = bf16[144,1152]{1,0:T(8,128)(2,1)S(1)} collective-permute-done((bf16[144,1152]{1,0:T(8,128)(2,1)S(1)}, bf16[144,1152]{1,0:T(8,128)(2,1)S(1)}, u32[]{:S(2)}, u32[]{:S(2)}) %collective-permute-start.13) | collective-permute-done | bytes 331808 | tf_op jit(solution)/shard_map/ppermute | solution.py:406
  46.5 1.3 %collective-permute-start.4 = (bf16[2,5,112,112]{3,2,1,0:T(8,128)(2,1)S(1)}, bf16[2,5,112,112]{3,2,1,0:T(8,128)(2,1)S(1)}, u32[]{:S(2)}, u32[]{:S(2)}) collective-permute-start(bf16[2,5,112,112]{3,2,1,0:T(8,128)(2,1)S(1)} %get-tuple-element.16), channel_id=1, source_target_pairs={{0,4},{4,8},{8,12},{1,5},{5,9},{9,13},{2,6},{6,10},{10,14},{3,7},{... | collective-permute-start | bytes 752648 | tf_op jit(solution)/shard_map/ppermute | solution.py:453
  47.8 3.7 %collective-permute-start.20 = (bf16[144,1152]{1,0:T(8,128)(2,1)S(1)}, bf16[144,1152]{1,0:T(8,128)(2,1)S(1)}, u32[]{:S(2)}, u32[]{:S(2)}) collective-permute-start(bf16[144,1152]{1,0:T(8,128)(2,1)S(1)} %collective-permute-done.19.rest_15_), channel_id=1, source_target_pairs={{0,1},{1,0},{2,3},{3,2},{4,5},{5,4},{6,7},{7,6},{8,9},{9,8},{10,11... | collective-permute-start | bytes 995336 | tf_op jit(solution)/shard_map/ppermute | solution.py:409
  51.5 0.7 copy-done.17
  52.2 1.2 %collective-permute-start.29 = (bf16[144,1152]{1,0:T(8,128)(2,1)S(1)}, bf16[144,1152]{1,0:T(8,128)(2,1)S(1)}, u32[]{:S(2)}, u32[]{:S(2)}) collective-permute-start(bf16[144,1152]{1,0:T(8,128)(2,1)S(1)} %collective-permute-done.25.rest_21_), channel_id=1, source_target_pairs={{0,16},{16,0},{1,17},{17,1},{2,18},{18,2},{3,19},{19,3},{4,20},{20... | collective-permute-start | bytes 995336 | tf_op jit(solution)/shard_map/ppermute | solution.py:403
  53.4 0.7 copy-done.19
  54.2 1.2 %collective-permute-start.27 = (bf16[144,1152]{1,0:T(8,128)(2,1)S(1)}, bf16[144,1152]{1,0:T(8,128)(2,1)}, u32[]{:S(2)}, u32[]{:S(2)}) collective-permute-start(bf16[144,1152]{1,0:T(8,128)(2,1)S(1)} %collective-permute-done.25.rest_21_), channel_id=1, source_target_pairs={{0,2},{1,3},{2,0},{3,1},{4,6},{5,7},{6,4},{7,5},{8,10},{9,11},{10,... | collective-permute-start | bytes 995336 | tf_op jit(solution)/shard_map/ppermute | solution.py:406
  55.4 0.6 collective-permute-start.26
  56.0 2.6 %collective-permute-start.14 = (bf16[144,1152]{1,0:T(8,128)(2,1)S(1)}, bf16[144,1152]{1,0:T(8,128)(2,1)S(1)}, u32[]{:S(2)}, u32[]{:S(2)}) collective-permute-start(bf16[144,1152]{1,0:T(8,128)(2,1)S(1)} %collective-permute-done.13.rest_9_), channel_id=1, source_target_pairs={{0,1},{1,0},{2,3},{3,2},{4,5},{5,4},{6,7},{7,6},{8,9},{9,8},{10,11... | collective-permute-start | bytes 995336 | tf_op jit(solution)/shard_map/ppermute | solution.py:409
  58.6 0.7 shard_map.75
  59.3 1.3 %collective-permute-start.5 = (bf16[2,5,112,112]{3,2,1,0:T(8,128)(2,1)S(1)}, bf16[2,5,112,112]{3,2,1,0:T(8,128)(2,1)S(1)}, u32[]{:S(2)}, u32[]{:S(2)}) collective-permute-start(bf16[2,5,112,112]{3,2,1,0:T(8,128)(2,1)S(1)} %shard_map.75), channel_id=1, source_target_pairs={{0,8},{4,12},{1,9},{5,13},{2,10},{6,14},{3,11},{7,15},{16,24},{20,... | collective-permute-start | bytes 752648 | tf_op jit(solution)/shard_map/ppermute | solution.py:453
  60.6 1.0 collective-permute-done.29.rest_25_
  61.6 1.2 %collective-permute-start.15 = (bf16[144,1152]{1,0:T(8,128)(2,1)S(1)}, bf16[144,1152]{1,0:T(8,128)(2,1)}, u32[]{:S(2)}, u32[]{:S(2)}) collective-permute-start(bf16[144,1152]{1,0:T(8,128)(2,1)S(1)} %collective-permute-done.11.rest_7_), channel_id=1, source_target_pairs={{0,2},{1,3},{2,0},{3,1},{4,6},{5,7},{6,4},{7,5},{8,10},{9,11},{10,... | collective-permute-start | bytes 995336 | tf_op jit(solution)/shard_map/ppermute | solution.py:406
  62.8 0.5 collective-permute-done.27.rest_23_
  63.3 1.2 collective-permute-start.12
  64.6 0.7 collective-permute-start.31
  65.2 11.4 %collective-permute-done.5.rest_1_ = bf16[2,5,112,112]{3,2,1,0:T(8,128)(2,1)S(1)} collective-permute-done((bf16[2,5,112,112]{3,2,1,0:T(8,128)(2,1)S(1)}, bf16[2,5,112,112]{3,2,1,0:T(8,128)(2,1)S(1)}, u32[]{:S(2)}, u32[]{:S(2)}) %collective-permute-start.5) | collective-permute-done | bytes 250912 | tf_op jit(solution)/shard_map/ppermute | solution.py:453
  76.6 0.4 collective-permute-start.30
  77.1 0.8 shard_map.76.rest_0_
  77.8 1.2 %collective-permute-start.7 = (bf16[2,5,112,112]{3,2,1,0:T(8,128)(2,1)S(1)}, bf16[2,5,112,112]{3,2,1,0:T(8,128)(2,1)}, u32[]{:S(2)}, u32[]{:S(2)}) collective-permute-start(bf16[2,5,112,112]{3,2,1,0:T(8,128)(2,1)S(1)} %shard_map.76.rest_0_), channel_id=1, source_target_pairs={{0,2},{1,3},{2,0},{3,1},{4,6},{5,7},{6,4},{7,5},{8,10},{9,11},{10,... | collective-permute-start | bytes 752648 | tf_op jit(solution)/shard_map/ppermute | solution.py:466
  79.1 0.7 copy-done.31
  80.2 0.7 copy-done.33
  81.4 0.8 copy-done.35
  82.4 4.0 %collective-permute-done.7.rest_2_ = bf16[2,5,112,112]{3,2,1,0:T(8,128)(2,1)} collective-permute-done((bf16[2,5,112,112]{3,2,1,0:T(8,128)(2,1)S(1)}, bf16[2,5,112,112]{3,2,1,0:T(8,128)(2,1)}, u32[]{:S(2)}, u32[]{:S(2)}) %collective-permute-start.7) | collective-permute-done | bytes 250912 | tf_op jit(solution)/shard_map/ppermute | solution.py:466
  86.4 1.0 collective-permute-start.8
  87.5 1.4 %collective-permute-done.8.rest_3_ = bf16[2,5,112,112]{3,2,1,0:T(8,128)(2,1)} collective-permute-done((bf16[2,5,112,112]{3,2,1,0:T(8,128)(2,1)}, bf16[2,5,112,112]{3,2,1,0:T(8,128)(2,1)}, u32[]{:S(2)}, u32[]{:S(2)}) %collective-permute-start.8) | collective-permute-done | bytes 250912 | tf_op jit(solution)/shard_map/ppermute | solution.py:469
  89.0 1.6 %copy-done.4 = bf16[2,2,128,2240]{2,3,1,0:T(8,128)(2,1)S(1)} copy-done((bf16[2,2,128,2240]{2,3,1,0:T(8,128)(2,1)S(1)}, bf16[2,2,128,2240]{2,3,1,0:T(8,128)(2,1)}, u32[]{:S(2)}) %copy-start.4) | copy-done | bytes 2293784
  90.6 1.0 copy-done.6
  91.6 1.0 copy-done.8
  92.6 1.0 copy-done.10
  93.5 1.0 copy-done.12
  94.5 1.0 copy-done.14
  95.5 1.0 copy-done.16
  96.5 1.0 copy-done.18
  97.4 1.0 copy-done.20
  98.4 1.0 copy-done.22
  99.4 1.0 copy-done.24
  100.3 1.0 copy-done.26
  101.3 1.0 copy-done.28
  102.3 1.0 copy-done.30
  103.3 1.0 copy-done.32
  104.2 1.0 copy-done.34
  105.2 1.0 copy-done.36
  106.2 11.0 %project.1 = bf16[2,2,2240,128]{3,2,1,0:T(8,128)(2,1)} custom-call(bf16[2,2,2240,128]{3,2,1,0:T(8,128)(2,1)S(1)} %bitcast.4, f32[20,112]{1,0:T(8,128)S(1)} %reshape.3.gain_ref, bf16[2,5,112,112]{3,2,1,0:T(8,128)(2,1)S(1)} %shard_map.76.rest_0_, bf16[2,5,112,112]{3,2,1,0:T(8,128)(2,1)} %collective-permute-done.6.rest_1_, ...), custom_call_target="tpu_custom_call" | custom-call | flops 6165626880 | bytes 14622720 | tf_op jit(solution)/shard_map/project/pallas_call | solution.py:310
  (88 shorter events, 2.2 us)
Async XLA Ops:
  1.9 10.8 %collective-permute-start.17 = (bf16[144,1152]{1,0:T(8,128)(2,1)}, bf16[144,1152]{1,0:T(8,128)(2,1)S(1)}, u32[]{:S(2)}, u32[]{:S(2)}) collective-permute-start(bf16[144,1152]{1,0:T(8,128)(2,1)} %cut.1), channel_id=1, source_target_pairs={{0,12},{4,0},{8,4},{12,8},{1,13},{5,1},{9,5},{13,9},{2,14},{6,2},{... | collective-permute-start | bytes 995336 | tf_op jit(solution)/shard_map/ppermute | solution.py:396
  2.1 5.5 %copy-start.37 = (bf16[144,1152]{1,0:T(8,128)(2,1)S(1)}, bf16[144,1152]{1,0:T(8,128)(2,1)}, u32[]{:S(2)}) copy-start(bf16[144,1152]{1,0:T(8,128)(2,1)} %cut.1) | copy-start | bytes 995332
  2.1 19.7 %copy-start.3 = (s32[2]{0:T(128)S(1)}, s32[2]{0:T(128)}, u32[]{:S(2)}) copy-start(s32[2]{0:T(128)} %blocks.5) | copy-start | bytes 28
  2.1 39.0 %copy-start.2 = (s32[2]{0:T(128)S(1)}, s32[2]{0:T(128)}, u32[]{:S(2)}) copy-start(s32[2]{0:T(128)} %flags.5) | copy-start | bytes 28
  6.6 15.2 %collective-permute-start.2 = (bf16[2,2,5,112,112]{4,3,2,1,0:T(8,128)(2,1)}, bf16[2,2,5,112,112]{4,3,2,1,0:T(8,128)(2,1)S(1)}, u32[]{:S(2)}, u32[]{:S(2)}) collective-permute-start(bf16[2,2,5,112,112]{4,3,2,1,0:T(8,128)(2,1)} %get-tuple-element.12), channel_id=1, source_target_pairs={{0,1},{1,0},{2,3},{3,2},{4,5},{5,4},{6,7},{7,6},{8,9},{9,8},{10,11... | collective-permute-start | bytes 1505288 | tf_op jit(solution)/shard_map/ppermute | solution.py:446
  7.6 13.1 %collective-permute-start.9 = (bf16[144,1152]{1,0:T(8,128)(2,1)S(1)}, bf16[144,1152]{1,0:T(8,128)(2,1)S(1)}, u32[]{:S(2)}, u32[]{:S(2)}) collective-permute-start(bf16[144,1152]{1,0:T(8,128)(2,1)S(1)} %copy-done.37), channel_id=1, source_target_pairs={{0,4},{4,8},{8,12},{12,0},{1,5},{5,9},{9,13},{13,1},{2,6},{6,10},{... | collective-permute-start | bytes 995336 | tf_op jit(solution)/shard_map/ppermute | solution.py:396
  12.6 22.3 %collective-permute-start.21 = (bf16[144,1152]{1,0:T(8,128)(2,1)S(1)}, bf16[144,1152]{1,0:T(8,128)(2,1)S(1)}, u32[]{:S(2)}, u32[]{:S(2)}) collective-permute-start(bf16[144,1152]{1,0:T(8,128)(2,1)S(1)} %collective-permute-done.17.rest_13_), channel_id=1, source_target_pairs={{0,16},{16,0},{1,17},{17,1},{2,18},{18,2},{3,19},{19,3},{4,20},{20... | collective-permute-start | bytes 995336 | tf_op jit(solution)/shard_map/ppermute | solution.py:403
  13.9 21.3 %collective-permute-start.19 = (bf16[144,1152]{1,0:T(8,128)(2,1)S(1)}, bf16[144,1152]{1,0:T(8,128)(2,1)S(1)}, u32[]{:S(2)}, u32[]{:S(2)}) collective-permute-start(bf16[144,1152]{1,0:T(8,128)(2,1)S(1)} %collective-permute-done.17.rest_13_), channel_id=1, source_target_pairs={{0,2},{1,3},{2,0},{3,1},{4,6},{5,7},{6,4},{7,5},{8,10},{9,11},{10,... | collective-permute-start | bytes 995336 | tf_op jit(solution)/shard_map/ppermute | solution.py:406
  15.1 21.4 %collective-permute-start.18 = (bf16[144,1152]{1,0:T(8,128)(2,1)S(1)}, bf16[144,1152]{1,0:T(8,128)(2,1)S(1)}, u32[]{:S(2)}, u32[]{:S(2)}) collective-permute-start(bf16[144,1152]{1,0:T(8,128)(2,1)S(1)} %collective-permute-done.17.rest_13_), channel_id=1, source_target_pairs={{0,1},{1,0},{2,3},{3,2},{4,5},{5,4},{6,7},{7,6},{8,9},{9,8},{10,11... | collective-permute-start | bytes 995336 | tf_op jit(solution)/shard_map/ppermute | solution.py:409
  20.7 20.0 %collective-permute-start.25 = (bf16[144,1152]{1,0:T(8,128)(2,1)S(1)}, bf16[144,1152]{1,0:T(8,128)(2,1)S(1)}, u32[]{:S(2)}, u32[]{:S(2)}) collective-permute-start(bf16[144,1152]{1,0:T(8,128)(2,1)S(1)} %collective-permute-done.9.rest_5_), channel_id=1, source_target_pairs={{0,4},{4,8},{8,12},{12,0},{1,5},{5,9},{9,13},{13,1},{2,6},{6,10},{... | collective-permute-start | bytes 995336 | tf_op jit(solution)/shard_map/ppermute | solution.py:396
  21.8 7.6 %collective-permute-start.1 = (s32[2]{0:T(128)S(1)}, s32[2]{0:T(128)S(1)}, u32[]{:S(2)}, u32[]{:S(2)}) collective-permute-start(s32[2]{0:T(128)S(1)} %copy-done.3), channel_id=1, source_target_pairs={{0,8},{4,12},{1,9},{5,13},{2,10},{6,14},{3,11},{7,15},{16,24},{20,... | collective-permute-start | bytes 32 | tf_op jit(solution)/shard_map/ppermute | solution.py:462
  23.1 1.3 %copy-start.1 = (f32[2,2,5,112,112]{4,3,2,1,0:T(8,128)S(1)}, f32[2,2,5,112,112]{4,3,2,1,0:T(8,128)}, u32[]{:S(2)}) copy-start(f32[2,2,5,112,112]{4,3,2,1,0:T(8,128)} %get-tuple-element.11.own_ref) | copy-start | bytes 3010564
  24.3 63.1 %copy-start.38 = (f32[2240]{0:T(1024)S(1)}, f32[2240]{0:T(1024)}, u32[]{:S(2)}) copy-start(f32[2240]{0:T(1024)} %param.13) | copy-start | bytes 26884
  24.3 64.6 %copy-start = (bf16[560,2240]{1,0:T(8,128)(2,1)S(1)}, bf16[560,2240]{1,0:T(8,128)(2,1)}, u32[]{:S(2)}) copy-start(bf16[560,2240]{1,0:T(8,128)(2,1)} %rest_4_.1) | copy-start | bytes 7526404
  29.4 4.3 %collective-permute-start = (s32[2]{0:T(128)S(1)}, s32[2]{0:T(128)S(1)}, u32[]{:S(2)}, u32[]{:S(2)}) collective-permute-start(s32[2]{0:T(128)S(1)} %copy-done.3), channel_id=1, source_target_pairs={{0,4},{4,8},{8,12},{1,5},{5,9},{9,13},{2,6},{6,10},{10,14},{3,7},{... | collective-permute-start | bytes 32 | tf_op jit(solution)/shard_map/ppermute | solution.py:448
  33.7 7.1 %collective-permute-start.3 = (bf16[2,5,112,112]{3,2,1,0:T(8,128)(2,1)S(1)}, bf16[2,5,112,112]{3,2,1,0:T(8,128)(2,1)S(1)}, u32[]{:S(2)}, u32[]{:S(2)}) collective-permute-start(bf16[2,5,112,112]{3,2,1,0:T(8,128)(2,1)S(1)} %get-tuple-element.14), channel_id=1, source_target_pairs={{0,2},{1,3},{2,0},{3,1},{4,6},{5,7},{6,4},{7,5},{8,10},{9,11},{10,... | collective-permute-start | bytes 752648 | tf_op jit(solution)/shard_map/ppermute | solution.py:447
  34.9 51.4 %copy-start.5 = (bf16[144,1152]{1,0:T(8,128)(2,1)}, bf16[144,1152]{1,0:T(8,128)(2,1)S(1)}, u32[]{:S(2)}) copy-start(bf16[144,1152]{1,0:T(8,128)(2,1)S(1)} %collective-permute-done.21.rest_17_) | copy-start | bytes 995332
  35.0 11.5 %collective-permute-start.13 = (bf16[144,1152]{1,0:T(8,128)(2,1)S(1)}, bf16[144,1152]{1,0:T(8,128)(2,1)S(1)}, u32[]{:S(2)}, u32[]{:S(2)}) collective-permute-start(bf16[144,1152]{1,0:T(8,128)(2,1)S(1)} %collective-permute-done.9.rest_5_), channel_id=1, source_target_pairs={{0,2},{1,3},{2,0},{3,1},{4,6},{5,7},{6,4},{7,5},{8,10},{9,11},{10,... | collective-permute-start | bytes 995336 | tf_op jit(solution)/shard_map/ppermute | solution.py:406
  35.2 51.1 %copy-start.7 = (bf16[144,1152]{1,0:T(8,128)(2,1)}, bf16[144,1152]{1,0:T(8,128)(2,1)S(1)}, u32[]{:S(2)}) copy-start(bf16[144,1152]{1,0:T(8,128)(2,1)S(1)} %collective-permute-done.19.rest_15_) | copy-start | bytes 995332
  35.2 12.6 %collective-permute-start.11 = (bf16[144,1152]{1,0:T(8,128)(2,1)S(1)}, bf16[144,1152]{1,0:T(8,128)(2,1)S(1)}, u32[]{:S(2)}, u32[]{:S(2)}) collective-permute-start(bf16[144,1152]{1,0:T(8,128)(2,1)S(1)} %collective-permute-done.9.rest_5_), channel_id=1, source_target_pairs={{0,16},{16,0},{1,17},{17,1},{2,18},{18,2},{3,19},{19,3},{4,20},{20... | collective-permute-start | bytes 995336 | tf_op jit(solution)/shard_map/ppermute | solution.py:403
  37.2 14.3 %collective-permute-start.10 = (bf16[144,1152]{1,0:T(8,128)(2,1)S(1)}, bf16[144,1152]{1,0:T(8,128)(2,1)S(1)}, u32[]{:S(2)}, u32[]{:S(2)}) collective-permute-start(bf16[144,1152]{1,0:T(8,128)(2,1)S(1)} %collective-permute-done.9.rest_5_), channel_id=1, source_target_pairs={{0,1},{1,0},{2,3},{3,2},{4,5},{5,4},{6,7},{7,6},{8,9},{9,8},{10,11... | collective-permute-start | bytes 995336 | tf_op jit(solution)/shard_map/ppermute | solution.py:409
  40.8 45.6 %copy-start.11 = (bf16[144,1152]{1,0:T(8,128)(2,1)}, bf16[144,1152]{1,0:T(8,128)(2,1)S(1)}, u32[]{:S(2)}) copy-start(bf16[144,1152]{1,0:T(8,128)(2,1)S(1)} %collective-permute-done.25.rest_21_) | copy-start | bytes 995332
  40.8 12.7 %collective-permute-start.22 = (bf16[144,1152]{1,0:T(8,128)(2,1)S(1)}, bf16[144,1152]{1,0:T(8,128)(2,1)S(1)}, u32[]{:S(2)}, u32[]{:S(2)}) collective-permute-start(bf16[144,1152]{1,0:T(8,128)(2,1)S(1)} %collective-permute-done.21.rest_17_), channel_id=1, source_target_pairs={{0,1},{1,0},{2,3},{3,2},{4,5},{5,4},{6,7},{7,6},{8,9},{9,8},{10,11... | collective-permute-start | bytes 995336 | tf_op jit(solution)/shard_map/ppermute | solution.py:409
  40.9 14.5 %collective-permute-start.23 = (bf16[144,1152]{1,0:T(8,128)(2,1)S(1)}, bf16[144,1152]{1,0:T(8,128)(2,1)S(1)}, u32[]{:S(2)}, u32[]{:S(2)}) collective-permute-start(bf16[144,1152]{1,0:T(8,128)(2,1)S(1)} %collective-permute-done.19.rest_15_), channel_id=1, source_target_pairs={{0,16},{16,0},{1,17},{17,1},{2,18},{18,2},{3,19},{19,3},{4,20},{20... | collective-permute-start | bytes 995336 | tf_op jit(solution)/shard_map/ppermute | solution.py:403
  46.5 39.9 %copy-start.13 = (bf16[144,1152]{1,0:T(8,128)(2,1)}, bf16[144,1152]{1,0:T(8,128)(2,1)S(1)}, u32[]{:S(2)}) copy-start(bf16[144,1152]{1,0:T(8,128)(2,1)S(1)} %collective-permute-done.13.rest_9_) | copy-start | bytes 995332
  46.5 9.5 %collective-permute-start.4 = (bf16[2,5,112,112]{3,2,1,0:T(8,128)(2,1)S(1)}, bf16[2,5,112,112]{3,2,1,0:T(8,128)(2,1)S(1)}, u32[]{:S(2)}, u32[]{:S(2)}) collective-permute-start(bf16[2,5,112,112]{3,2,1,0:T(8,128)(2,1)S(1)} %get-tuple-element.16), channel_id=1, source_target_pairs={{0,4},{4,8},{8,12},{1,5},{5,9},{9,13},{2,6},{6,10},{10,14},{3,7},{... | collective-permute-start | bytes 752648 | tf_op jit(solution)/shard_map/ppermute | solution.py:453
  47.8 38.6 %copy-start.15 = (bf16[144,1152]{1,0:T(8,128)(2,1)}, bf16[144,1152]{1,0:T(8,128)(2,1)S(1)}, u32[]{:S(2)}) copy-start(bf16[144,1152]{1,0:T(8,128)(2,1)S(1)} %collective-permute-done.11.rest_7_) | copy-start | bytes 995332
  47.8 11.5 %collective-permute-start.20 = (bf16[144,1152]{1,0:T(8,128)(2,1)S(1)}, bf16[144,1152]{1,0:T(8,128)(2,1)S(1)}, u32[]{:S(2)}, u32[]{:S(2)}) collective-permute-start(bf16[144,1152]{1,0:T(8,128)(2,1)S(1)} %collective-permute-done.19.rest_15_), channel_id=1, source_target_pairs={{0,1},{1,0},{2,3},{3,2},{4,5},{5,4},{6,7},{7,6},{8,9},{9,8},{10,11... | collective-permute-start | bytes 995336 | tf_op jit(solution)/shard_map/ppermute | solution.py:409
  52.2 9.4 %collective-permute-start.29 = (bf16[144,1152]{1,0:T(8,128)(2,1)S(1)}, bf16[144,1152]{1,0:T(8,128)(2,1)S(1)}, u32[]{:S(2)}, u32[]{:S(2)}) collective-permute-start(bf16[144,1152]{1,0:T(8,128)(2,1)S(1)} %collective-permute-done.25.rest_21_), channel_id=1, source_target_pairs={{0,16},{16,0},{1,17},{17,1},{2,18},{18,2},{3,19},{19,3},{4,20},{20... | collective-permute-start | bytes 995336 | tf_op jit(solution)/shard_map/ppermute | solution.py:403
  54.2 9.2 %collective-permute-start.27 = (bf16[144,1152]{1,0:T(8,128)(2,1)S(1)}, bf16[144,1152]{1,0:T(8,128)(2,1)}, u32[]{:S(2)}, u32[]{:S(2)}) collective-permute-start(bf16[144,1152]{1,0:T(8,128)(2,1)S(1)} %collective-permute-done.25.rest_21_), channel_id=1, source_target_pairs={{0,2},{1,3},{2,0},{3,1},{4,6},{5,7},{6,4},{7,5},{8,10},{9,11},{10,... | collective-permute-start | bytes 995336 | tf_op jit(solution)/shard_map/ppermute | solution.py:406
  55.4 31.0 %copy-start.21 = (bf16[144,1152]{1,0:T(8,128)(2,1)}, bf16[144,1152]{1,0:T(8,128)(2,1)S(1)}, u32[]{:S(2)}) copy-start(bf16[144,1152]{1,0:T(8,128)(2,1)S(1)} %collective-permute-done.23.rest_19_) | copy-start | bytes 995332
  55.4 9.1 %collective-permute-start.26 = (bf16[144,1152]{1,0:T(8,128)(2,1)S(1)}, bf16[144,1152]{1,0:T(8,128)(2,1)S(1)}, u32[]{:S(2)}, u32[]{:S(2)}) collective-permute-start(bf16[144,1152]{1,0:T(8,128)(2,1)S(1)} %collective-permute-done.25.rest_21_), channel_id=1, source_target_pairs={{0,1},{1,0},{2,3},{3,2},{4,5},{5,4},{6,7},{7,6},{8,9},{9,8},{10,11... | collective-permute-start | bytes 995336 | tf_op jit(solution)/shard_map/ppermute | solution.py:409
  56.0 8.6 %collective-permute-start.14 = (bf16[144,1152]{1,0:T(8,128)(2,1)S(1)}, bf16[144,1152]{1,0:T(8,128)(2,1)S(1)}, u32[]{:S(2)}, u32[]{:S(2)}) collective-permute-start(bf16[144,1152]{1,0:T(8,128)(2,1)S(1)} %collective-permute-done.13.rest_9_), channel_id=1, source_target_pairs={{0,1},{1,0},{2,3},{3,2},{4,5},{5,4},{6,7},{7,6},{8,9},{9,8},{10,11... | collective-permute-start | bytes 995336 | tf_op jit(solution)/shard_map/ppermute | solution.py:409
  59.3 27.0 %copy-start.23 = (bf16[144,1152]{1,0:T(8,128)(2,1)}, bf16[144,1152]{1,0:T(8,128)(2,1)S(1)}, u32[]{:S(2)}) copy-start(bf16[144,1152]{1,0:T(8,128)(2,1)S(1)} %collective-permute-done.20.rest_16_) | copy-start | bytes 995332
  59.3 17.3 %collective-permute-start.5 = (bf16[2,5,112,112]{3,2,1,0:T(8,128)(2,1)S(1)}, bf16[2,5,112,112]{3,2,1,0:T(8,128)(2,1)S(1)}, u32[]{:S(2)}, u32[]{:S(2)}) collective-permute-start(bf16[2,5,112,112]{3,2,1,0:T(8,128)(2,1)S(1)} %shard_map.75), channel_id=1, source_target_pairs={{0,8},{4,12},{1,9},{5,13},{2,10},{6,14},{3,11},{7,15},{16,24},{20,... | collective-permute-start | bytes 752648 | tf_op jit(solution)/shard_map/ppermute | solution.py:453
  61.6 24.8 %copy-start.25 = (bf16[144,1152]{1,0:T(8,128)(2,1)}, bf16[144,1152]{1,0:T(8,128)(2,1)S(1)}, u32[]{:S(2)}) copy-start(bf16[144,1152]{1,0:T(8,128)(2,1)S(1)} %collective-permute-done.29.rest_25_) | copy-start | bytes 995332
  61.6 16.2 %collective-permute-start.15 = (bf16[144,1152]{1,0:T(8,128)(2,1)S(1)}, bf16[144,1152]{1,0:T(8,128)(2,1)}, u32[]{:S(2)}, u32[]{:S(2)}) collective-permute-start(bf16[144,1152]{1,0:T(8,128)(2,1)S(1)} %collective-permute-done.11.rest_7_), channel_id=1, source_target_pairs={{0,2},{1,3},{2,0},{3,1},{4,6},{5,7},{6,4},{7,5},{8,10},{9,11},{10,... | collective-permute-start | bytes 995336 | tf_op jit(solution)/shard_map/ppermute | solution.py:406
  63.3 15.7 %collective-permute-start.12 = (bf16[144,1152]{1,0:T(8,128)(2,1)S(1)}, bf16[144,1152]{1,0:T(8,128)(2,1)S(1)}, u32[]{:S(2)}, u32[]{:S(2)}) collective-permute-start(bf16[144,1152]{1,0:T(8,128)(2,1)S(1)} %collective-permute-done.11.rest_7_), channel_id=1, source_target_pairs={{0,1},{1,0},{2,3},{3,2},{4,5},{5,4},{6,7},{7,6},{8,9},{9,8},{10,11... | collective-permute-start | bytes 995336 | tf_op jit(solution)/shard_map/ppermute | solution.py:409
  64.5 21.9 %copy-start.27 = (bf16[144,1152]{1,0:T(8,128)(2,1)}, bf16[144,1152]{1,0:T(8,128)(2,1)S(1)}, u32[]{:S(2)}) copy-start(bf16[144,1152]{1,0:T(8,128)(2,1)S(1)} %collective-permute-done.26.rest_22_) | copy-start | bytes 995332
  64.5 15.7 %collective-permute-start.24 = (bf16[144,1152]{1,0:T(8,128)(2,1)S(1)}, bf16[144,1152]{1,0:T(8,128)(2,1)S(1)}, u32[]{:S(2)}, u32[]{:S(2)}) collective-permute-start(bf16[144,1152]{1,0:T(8,128)(2,1)S(1)} %collective-permute-done.23.rest_19_), channel_id=1, source_target_pairs={{0,1},{1,0},{2,3},{3,2},{4,5},{5,4},{6,7},{7,6},{8,9},{9,8},{10,11... | collective-permute-start | bytes 995336 | tf_op jit(solution)/shard_map/ppermute | solution.py:409
  64.6 21.8 %copy-start.29 = (bf16[144,1152]{1,0:T(8,128)(2,1)}, bf16[144,1152]{1,0:T(8,128)(2,1)S(1)}, u32[]{:S(2)}) copy-start(bf16[144,1152]{1,0:T(8,128)(2,1)S(1)} %collective-permute-done.14.rest_10_) | copy-start | bytes 995332
  64.6 16.5 %collective-permute-start.31 = (bf16[144,1152]{1,0:T(8,128)(2,1)}, bf16[144,1152]{1,0:T(8,128)(2,1)}, u32[]{:S(2)}, u32[]{:S(2)}) collective-permute-start(bf16[144,1152]{1,0:T(8,128)(2,1)} %collective-permute-done.27.rest_23_), channel_id=1, source_target_pairs={{0,16},{16,0},{1,17},{17,1},{2,18},{18,2},{3,19},{19,3},{4,20},{20... | collective-permute-start | bytes 995336 | tf_op jit(solution)/shard_map/ppermute | solution.py:403
  76.6 4.8 %collective-permute-start.30 = (bf16[144,1152]{1,0:T(8,128)(2,1)S(1)}, bf16[144,1152]{1,0:T(8,128)(2,1)S(1)}, u32[]{:S(2)}, u32[]{:S(2)}) collective-permute-start(bf16[144,1152]{1,0:T(8,128)(2,1)S(1)} %collective-permute-done.29.rest_25_), channel_id=1, source_target_pairs={{0,1},{1,0},{2,3},{3,2},{4,5},{5,4},{6,7},{7,6},{8,9},{9,8},{10,11... | collective-permute-start | bytes 995336 | tf_op jit(solution)/shard_map/ppermute | solution.py:409
  77.8 8.5 %collective-permute-start.7 = (bf16[2,5,112,112]{3,2,1,0:T(8,128)(2,1)S(1)}, bf16[2,5,112,112]{3,2,1,0:T(8,128)(2,1)}, u32[]{:S(2)}, u32[]{:S(2)}) collective-permute-start(bf16[2,5,112,112]{3,2,1,0:T(8,128)(2,1)S(1)} %shard_map.76.rest_0_), channel_id=1, source_target_pairs={{0,2},{1,3},{2,0},{3,1},{4,6},{5,7},{6,4},{7,5},{8,10},{9,11},{10,... | collective-permute-start | bytes 752648 | tf_op jit(solution)/shard_map/ppermute | solution.py:466
  79.8 7.7 %collective-permute-start.28 = (bf16[144,1152]{1,0:T(8,128)(2,1)}, bf16[144,1152]{1,0:T(8,128)(2,1)}, u32[]{:S(2)}, u32[]{:S(2)}) collective-permute-start(bf16[144,1152]{1,0:T(8,128)(2,1)} %collective-permute-done.27.rest_23_), channel_id=1, source_target_pairs={{0,1},{1,0},{2,3},{3,2},{4,5},{5,4},{6,7},{7,6},{8,9},{9,8},{10,11... | collective-permute-start | bytes 995336 | tf_op jit(solution)/shard_map/ppermute | solution.py:409
  80.9 6.6 %collective-permute-start.16 = (bf16[144,1152]{1,0:T(8,128)(2,1)}, bf16[144,1152]{1,0:T(8,128)(2,1)}, u32[]{:S(2)}, u32[]{:S(2)}) collective-permute-start(bf16[144,1152]{1,0:T(8,128)(2,1)} %collective-permute-done.15.rest_11_), channel_id=1, source_target_pairs={{0,1},{1,0},{2,3},{3,2},{4,5},{5,4},{6,7},{7,6},{8,9},{9,8},{10,11... | collective-permute-start | bytes 995336 | tf_op jit(solution)/shard_map/ppermute | solution.py:409
  81.1 6.4 %collective-permute-start.32 = (bf16[144,1152]{1,0:T(8,128)(2,1)}, bf16[144,1152]{1,0:T(8,128)(2,1)}, u32[]{:S(2)}, u32[]{:S(2)}) collective-permute-start(bf16[144,1152]{1,0:T(8,128)(2,1)} %collective-permute-done.31.rest_27_), channel_id=1, source_target_pairs={{0,1},{1,0},{2,3},{3,2},{4,5},{5,4},{6,7},{7,6},{8,9},{9,8},{10,11... | collective-permute-start | bytes 995336 | tf_op jit(solution)/shard_map/ppermute | solution.py:409
  82.2 5.3 %collective-permute-start.6 = (bf16[2,5,112,112]{3,2,1,0:T(8,128)(2,1)S(1)}, bf16[2,5,112,112]{3,2,1,0:T(8,128)(2,1)}, u32[]{:S(2)}, u32[]{:S(2)}) collective-permute-start(bf16[2,5,112,112]{3,2,1,0:T(8,128)(2,1)S(1)} %shard_map.76.rest_0_), channel_id=1, source_target_pairs={{0,1},{1,0},{2,3},{3,2},{4,5},{5,4},{6,7},{7,6},{8,9},{9,8},{10,11... | collective-permute-start | bytes 752648 | tf_op jit(solution)/shard_map/ppermute | solution.py:469
  86.4 2.5 %collective-permute-start.8 = (bf16[2,5,112,112]{3,2,1,0:T(8,128)(2,1)}, bf16[2,5,112,112]{3,2,1,0:T(8,128)(2,1)}, u32[]{:S(2)}, u32[]{:S(2)}) collective-permute-start(bf16[2,5,112,112]{3,2,1,0:T(8,128)(2,1)} %collective-permute-done.7.rest_2_), channel_id=1, source_target_pairs={{0,1},{1,0},{2,3},{3,2},{4,5},{5,4},{6,7},{7,6},{8,9},{9,8},{10,11... | collective-permute-start | bytes 752648 | tf_op jit(solution)/shard_map/ppermute | solution.py:469
  89.0 1.6 %copy-start.4 = (bf16[2,2,128,2240]{2,3,1,0:T(8,128)(2,1)S(1)}, bf16[2,2,128,2240]{2,3,1,0:T(8,128)(2,1)}, u32[]{:S(2)}) copy-start(bf16[2,2,128,2240]{2,3,1,0:T(8,128)(2,1)} %param.7) | copy-start | bytes 6881284
  90.6 1.0 copy-start.6
  91.6 1.0 copy-start.8
  92.5 1.0 copy-start.10
  93.5 1.0 copy-start.12
  94.5 1.0 copy-start.14
  95.5 1.0 copy-start.16
  96.4 1.0 copy-start.18
  97.4 1.0 copy-start.20
  98.4 1.0 copy-start.22
  99.4 1.0 copy-start.24
  100.3 1.0 copy-start.26
  101.3 1.0 copy-start.28
  104.2 1.0 copy-start.34
  105.2 1.0 copy-start.36
  (8 other events, 6.4 us)
